TPU v7x, 32 devices: a whole 2x2x4 slice. The times are simulated.
32 devices in a mesh: gz: 4 (over y, x), gy: 2 (over core), gx: 4 (over z).
Axes of the slice: x: 2, y: 2, z: 4, core: 2. Of those that a mesh axis runs over, the one named last changes fastest.
Arguments:
- vectors: bfloat16 [4, 2, 4, 4, 24, 2, 4, 3, 256], P('gz', 'gy', 'gx'), may hold values from -6 to 6
- links: bfloat16 [4, 2, 4, 4, 4, 2, 3, 3, 256], P('gz', 'gy', 'gx'), may hold values from -2.5 to 2.5
- site_term: bfloat16 [4, 2, 4, 4, 2, 2, 6, 6, 256], P('gz', 'gy', 'gx'), may hold values from -3 to 3, as said below
- owner: int32 [4, 2, 4, 4], replicated, may hold values from 0 to 15, as said below
- coarse_rhs: bfloat16 [4, 2, 4, 4, 2, 24], P('gz', 'gy', 'gx'), may hold values from -50 to 50
Outputs:
- coarse_operator: bfloat16 [16, 32, 9, 2, 576], P(('gz', 'gx'))
- coarse_solution: float32 [16, 32, 2, 24], P(('gz', 'gx'))
Inputs may be any that keep to these rules, and one draw needn't show every extreme that they name: Within each block of 4 aggregates with the same z, y, x no owner appears more than 1 times, and one owner appears exactly 1 times in every block. `site_term`: each chirality block is Hermitian.
All inputs are finite; a program needn't handle non-finite values.
Results may differ from a plain program's by a relative error of at most 0.009.
Values may be sent and summed in bfloat16 or wider, within the bound.
A program may use at most 128 MiB of HBM per device.

v0:
```python
import jax
import jax.numpy as jnp
import numpy as np
from jax import lax
from jax.experimental import pallas as pl
from jax.experimental.pallas import tpu as pltpu
from jax.sharding import PartitionSpec as P

NV = 24
AT = 4
ITERS = 4
PAIR = 1
LANES = 128
SLAB = 2 * NV * NV


coarse_scale = 1.0 / 256.0
epsilon = 1e-06
site_strides = (64, 16, 4, 1)
neighbor_offsets = (
    (0, 0, 0, 0),
    (0, 0, 1, 0),
    (0, 0, -1, 0),
    (0, 1, 0, 0),
    (0, -1, 0, 0),
    (1, 0, 0, 0),
    (-1, 0, 0, 0),
    (0, 0, 0, 1),
    (0, 0, 0, -1),
)


lower_table = (
    (((1, 3, 1), (0, 3, -1)), ((1, 2, 1), (0, 2, -1))),
    (((0, 3, -1), (1, 3, -1)), ((0, 2, 1), (1, 2, 1))),
    (((1, 2, 1), (0, 2, -1)), ((1, 3, -1), (0, 3, 1))),
    (((0, 2, 1), (1, 2, 1)), ((0, 3, 1), (1, 3, 1))),
)


def from_behind(block, axis, distance):
    devices = range(lax.axis_size(axis))
    route = [((i - distance) % len(devices), i) for i in devices]
    return lax.ppermute(block, axis, route)


def rounded(value):
    return value.astype(jnp.bfloat16).astype(jnp.float32)


def half(vec_ref, direction, spin, colour, sign):
    pair = []
    for part in range(2):
        from_part, from_spin, factor = lower_table[direction][spin][part]
        upper = vec_ref[0, part * 12 + spin * 3 + colour].astype(jnp.float32)
        lower = vec_ref[0, from_part * 12 + from_spin * 3 + colour].astype(jnp.float32)
        pair.append(rounded(upper + (sign * factor) * lower))
    return pair


def link(link_ref, direction, part, row, col):
    at = direction * 18 + part * 9 + row * 3 + col
    return link_ref[0, at : at + 1, :]


def halves_kernel(vec_ref, link_ref, minus_ref, back_ref):
    for mu in range(4):
        for spin in range(2):
            plus = []
            for col in range(3):
                minus = half(vec_ref, mu, spin, col, -1)
                plus.append(half(vec_ref, mu, spin, col, 1))
                for part in range(2):
                    minus_ref[mu, 0, part * 6 + spin * 3 + col] = minus[part].astype(jnp.bfloat16)
            for col in range(3):
                out_re, out_im = 0.0, 0.0
                for row in range(3):
                    u_re = link(link_ref, mu, 0, row, col)
                    u_im = link(link_ref, mu, 1, row, col)
                    p_re, p_im = plus[row]
                    out_re = out_re + u_re * p_re + u_im * p_im
                    out_im = out_im + u_re * p_im - u_im * p_re
                back_ref[mu, 0, spin * 3 + col] = out_re.astype(jnp.bfloat16)
                back_ref[mu, 0, 6 + spin * 3 + col] = out_im.astype(jnp.bfloat16)


def contract(left, right):
    return lax.dot_general(
        jnp.concatenate(left, axis=1),
        jnp.concatenate(right, axis=1),
        (((1,), (1,)), ((), ())),
        preferred_element_type=jnp.float32,
    )


def stacked(pieces):
    return jnp.concatenate(pieces, axis=0).astype(jnp.bfloat16)


def restrict_kernel(vec_ref, link_ref, site_ref, minus_ref, back_ref, *rest):
    near_minus, near_back, out_ref = rest[0:4], rest[4:8], rest[8]
    sites = vec_ref.shape[-1]
    left, right = [], []
    for chirality in range(2):
        for i in range(6):
            out_re, out_im = 0.0, 0.0
            for j in range(6):
                at = chirality * 72 + i * 6 + j
                m_re = site_ref[0, at : at + 1, :]
                m_im = site_ref[0, at + 36 : at + 37, :]
                v_re = vec_ref[0, chirality * 6 + j].astype(jnp.float32)
                v_im = vec_ref[0, 12 + chirality * 6 + j].astype(jnp.float32)
                out_re = out_re + m_re * v_re - m_im * v_im
                out_im = out_im + m_re * v_im + m_im * v_re
            right.append(stacked([out_re, out_im, out_re, out_im]))
            at = chirality * 6 + i
            left.append(
                stacked([vec_ref[0, at].astype(jnp.float32), vec_ref[0, 12 + at].astype(jnp.float32)])
            )
    out_ref[0, 0] = contract(left, right)
    position = lax.broadcasted_iota(jnp.int32, (NV, sites), 1)
    for mu in range(4):
        stride = site_strides[mu]
        coordinate = position // stride % 4
        last = coordinate == 3
        first = coordinate == 0

        def split(pair, edge):
            return stacked(
                [jnp.where(edge, 0.0, part) for part in pair]
                + [jnp.where(edge, part, 0.0) for part in pair]
            )

        def shifted(own, near, edge, own_shift, near_shift):
            return jnp.where(
                edge,
                pltpu.roll(near.astype(jnp.float32), near_shift, 1),
                pltpu.roll(own.astype(jnp.float32), own_shift, 1),
            )

        left, right = [], []
        for spin in range(2):
            field = []
            for col in range(3):
                at = spin * 3 + col
                field.append(
                    [
                        shifted(
                            minus_ref[mu, 0, part * 6 + at],
                            near_minus[mu][0, part * 6 + at],
                            last,
                            sites - stride,
                            3 * stride,
                        )
                        for part in range(2)
                    ]
                )
            for row in range(3):
                out_re, out_im = 0.0, 0.0
                for col in range(3):
                    u_re = link(link_ref, mu, 0, row, col)
                    u_im = link(link_ref, mu, 1, row, col)
                    f_re, f_im = field[col]
                    out_re = out_re + u_re * f_re - u_im * f_im
                    out_im = out_im + u_re * f_im + u_im * f_re
                right.append(split((out_re, out_im), last))
                at = spin * 3 + row
                left.append(
                    stacked([minus_ref[mu, 0, part * 6 + at].astype(jnp.float32) for part in range(2)])
                )
        out_ref[0, 2 * mu + 1] = contract(left, right)
        left, right = [], []
        for spin in range(2):
            for col in range(3):
                at = spin * 3 + col
                pair = [
                    shifted(
                        back_ref[mu, 0, part * 6 + at],
                        near_back[mu][0, part * 6 + at],
                        first,
                        stride,
                        sites - 3 * stride,
                    )
                    for part in range(2)
                ]
                right.append(split(pair, first))
                left.append(stacked(half(vec_ref, mu, spin, col, 1)))
        out_ref[0, 2 * mu + 2] = contract(left, right)


def fine_blocks(vectors, links, site_term):
    sites = vectors.shape[-1]
    vec = jnp.transpose(vectors, (0, 2, 3, 4, 1, 5)).reshape(AT, 24, NV, sites)
    link_f = links.astype(jnp.float32).reshape(AT, 72, sites)
    site_f = site_term.astype(jnp.float32).reshape(AT, 144, sites)
    vec_spec = pl.BlockSpec((1, 24, NV, sites), lambda a: (a, 0, 0, 0))
    link_spec = pl.BlockSpec((1, 72, sites), lambda a: (a, 0, 0))
    site_spec = pl.BlockSpec((1, 144, sites), lambda a: (a, 0, 0))
    half_spec = pl.BlockSpec((4, 1, 12, NV, sites), lambda a: (0, a, 0, 0, 0))
    near_spec = pl.BlockSpec((1, 12, NV, sites), lambda a: (a, 0, 0, 0))
    half_shape = jax.ShapeDtypeStruct((4, AT, 12, NV, sites), jnp.bfloat16)
    params = pltpu.CompilerParams(vmem_limit_bytes=48 << 20)
    minus, back = pl.pallas_call(
        halves_kernel,
        grid=(AT,),
        in_specs=[vec_spec, link_spec],
        out_specs=[half_spec, half_spec],
        out_shape=(half_shape, half_shape),
        compiler_params=params,
    )(vec, link_f)
    axes = ("gx", "gy", "gz")
    near_minus = [from_behind(minus[mu], axes[mu], -1) for mu in range(3)]
    near_back = [from_behind(back[mu], axes[mu], 1) for mu in range(3)]
    near_minus.append(jnp.roll(minus[3], -1, axis=0))
    near_back.append(jnp.roll(back[3], 1, axis=0))
    products = pl.pallas_call(
        restrict_kernel,
        grid=(AT,),
        in_specs=[vec_spec, link_spec, site_spec, half_spec, half_spec] + [near_spec] * 8,
        out_specs=pl.BlockSpec((1, 9, 2 * NV, 4 * NV), lambda a: (a, 0, 0, 0)),
        out_shape=jax.ShapeDtypeStruct((AT, 9, 2 * NV, 4 * NV), jnp.float32),
        compiler_params=params,
    )(vec, link_f, site_f, minus, back, *near_minus, *near_back)
    parts = products.reshape(AT, 9, 2, NV, 2, 2, NV)
    real = parts[:, :, 0, :, :, 0] + parts[:, :, 1, :, :, 1]
    imag = parts[:, :, 0, :, :, 1] - parts[:, :, 1, :, :, 0]
    both = jnp.stack([real, imag], 2)
    inside, outside = both[:, :, :, :, 0], both[:, :, :, :, 1]
    own = (inside[:, :1] - 0.5 * jnp.sum(inside[:, 1:], axis=1, keepdims=True)) * coarse_scale
    return jnp.concatenate([own, outside[:, 1:] * (-0.5 * coarse_scale)], axis=1)


def complex_mul(first, second):
    return (
        first[0] * second[0] - first[1] * second[1],
        first[0] * second[1] + first[1] * second[0],
    )


def rotate(top_entry, bottom_entry, scale_norm, upper_value, lower_value):
    conj_top = (top_entry[0], -top_entry[1])
    conj_bottom = (bottom_entry[0], -bottom_entry[1])
    part_one = complex_mul(conj_top, upper_value)
    part_two = complex_mul(conj_bottom, lower_value)
    part_three = complex_mul(bottom_entry, upper_value)
    part_four = complex_mul(top_entry, lower_value)
    new_upper = ((part_one[0] + part_two[0]) / scale_norm, (part_one[1] + part_two[1]) / scale_norm)
    new_lower = (
        (part_four[0] - part_three[0]) / scale_norm,
        (part_four[1] - part_three[1]) / scale_norm,
    )
    return (new_upper, new_lower)


def least_squares(hessen, beta):
    columns = len(hessen[0])
    zero_value = jnp.zeros((), jnp.float32)
    matrix = [list(row_list) for row_list in hessen]
    target = [(beta, zero_value)] + [(zero_value, zero_value)] * columns
    rotations = []
    for col_index in range(columns):
        for rot_index in range(col_index):
            top_entry, bottom_entry, scale_norm = rotations[rot_index]
            pair = rotate(
                top_entry,
                bottom_entry,
                scale_norm,
                matrix[rot_index][col_index],
                matrix[rot_index + 1][col_index],
            )
            matrix[rot_index][col_index] = pair[0]
            matrix[rot_index + 1][col_index] = pair[1]
        top_entry = matrix[col_index][col_index]
        bottom_entry = matrix[col_index + 1][col_index]
        scale_norm = jnp.sqrt(
            top_entry[0] * top_entry[0]
            + top_entry[1] * top_entry[1]
            + bottom_entry[0] * bottom_entry[0]
            + bottom_entry[1] * bottom_entry[1]
        )
        rotations.append((top_entry, bottom_entry, scale_norm))
        matrix[col_index][col_index] = (scale_norm, zero_value)
        matrix[col_index + 1][col_index] = (zero_value, zero_value)
        pair = rotate(top_entry, bottom_entry, scale_norm, target[col_index], target[col_index + 1])
        target[col_index] = pair[0]
        target[col_index + 1] = pair[1]
    weights = [None] * columns
    for row_index in reversed(range(columns)):
        remainder = target[row_index]
        for col_index in range(row_index + 1, columns):
            product_term = complex_mul(matrix[row_index][col_index], weights[col_index])
            remainder = (remainder[0] - product_term[0], remainder[1] - product_term[1])
        weights[row_index] = (
            remainder[0] / matrix[row_index][row_index][0],
            remainder[1] / matrix[row_index][row_index][0],
        )
    return weights


def split_two(value):
    high = value.astype(jnp.bfloat16)
    low = (value - high.astype(jnp.float32)).astype(jnp.bfloat16)
    return high, low


def turn(value):
    lane = lax.broadcasted_iota(jnp.int32, value.shape, 1)
    down = pltpu.roll(value, LANES - NV, 1)
    up = pltpu.roll(value, NV, 1)
    return jnp.where(lane < NV, down, jnp.where(lane < 2 * NV, -up, 0.0))


def total(value):
    return jnp.sum(jnp.sum(value, axis=0, keepdims=True), axis=1, keepdims=True)


def gmres_kernel(
    rows_ref, rhs_ref, perm_ref, expand_ref, reduce_ref, pick_ref, op_ref, sol_ref, near_ref, acc_ref
):
    count = rows_ref.shape[0]

    def apply(vector):
        high, low = split_two(vector)
        both = high.astype(jnp.float32) + pltpu.roll(low.astype(jnp.float32), 2 * NV, 1)
        both = both.astype(jnp.bfloat16)
        near_ref[...] = jnp.dot(
            perm_ref[...], both, preferred_element_type=jnp.float32
        ).astype(jnp.bfloat16)

        @pl.loop(0, SLAB // LANES)
        def _(chunk):
            at = pl.multiple_of(chunk * LANES, LANES)
            wide_at = pl.ds(pl.multiple_of(chunk * 2 * LANES, 2 * LANES), 2 * LANES)
            sums = jnp.zeros((count, 2 * LANES), jnp.float32)
            for k in range(9):
                near = near_ref[k * count : (k + 1) * count]
                rows = rows_ref[:, pl.ds(k * SLAB + at, LANES)].astype(jnp.float32)
                wide = jnp.dot(
                    near, expand_ref[:, wide_at], preferred_element_type=jnp.float32
                )
                sums = sums + jnp.concatenate([rows, rows], axis=1) * wide
            acc_ref[:, wide_at] = sums

        high, low = split_two(acc_ref[...])
        return jnp.dot(high, reduce_ref[...], preferred_element_type=jnp.float32) + jnp.dot(
            low, reduce_ref[...], preferred_element_type=jnp.float32
        )

    pick = pick_ref[...]
    for k in range(9):
        op_ref[:, k * SLAB : (k + 1) * SLAB] = jnp.dot(
            pick, rows_ref[:, k * SLAB : (k + 1) * SLAB], preferred_element_type=jnp.float32
        ).astype(jnp.bfloat16)
    right_side = rhs_ref[...]
    zero_value = jnp.zeros((1, 1), jnp.float32)
    beta = jnp.sqrt(total(right_side * right_side) + epsilon)
    basis = [right_side / beta]
    turned = [turn(basis[0])]
    hessen = []
    for row_index in range(ITERS + 1):
        hessen.append([(zero_value, zero_value)] * ITERS)
    for column in range(ITERS):
        work = apply(basis[column])
        for row_index in range(column + 1):
            coef_re = total(basis[row_index] * work)
            coef_im = -total(turned[row_index] * work)
            hessen[row_index][column] = (coef_re, coef_im)
            work = work - coef_re * basis[row_index] + coef_im * turned[row_index]
        norm_now = jnp.sqrt(total(work * work) + epsilon)
        hessen[column + 1][column] = (norm_now, zero_value)
        if column + 1 < ITERS:
            basis.append(work / norm_now)
            turned.append(turn(basis[-1]))
    weights = least_squares(hessen, beta)
    answer = jnp.zeros_like(right_side)
    for column in range(ITERS):
        answer = answer + weights[column][0] * basis[column] - weights[column][1] * turned[column]
    high, low = split_two(answer)
    rest = (answer - high.astype(jnp.float32) - low.astype(jnp.float32)).astype(jnp.bfloat16)
    sol_ref[...] = (
        jnp.dot(pick, high, preferred_element_type=jnp.float32)
        + jnp.dot(pick, low, preferred_element_type=jnp.float32)
        + jnp.dot(pick, rest, preferred_element_type=jnp.float32)
    )


def index_tables(size_z, size_y, size_x):
    count = size_z * size_y * size_x * AT
    where = np.arange(count).reshape(size_z, size_y, size_x, AT)
    perm = np.zeros((9, count, count), np.float32)
    for k, offset in enumerate(neighbor_offsets):
        source = np.roll(where, [-step for step in offset], axis=(0, 1, 2, 3)).reshape(-1)
        perm[k, np.arange(count), source] = 1.0
    lane = np.arange(SLAB)
    comp, row, col = lane // (NV * NV), lane // NV % NV, lane % NV
    expand = np.zeros((LANES, 2, SLAB), np.float32)
    reduce = np.zeros((2, SLAB, LANES), np.float32)
    for half in range(2):
        expand[half * NV + col, half, lane] = 1.0
        expand[(2 + half) * NV + col, half, lane] = 1.0
        out = np.where(comp == half, 0, NV) + row
        reduce[half, lane, out] = np.where((half == 1) & (comp == 1), -1.0, 1.0)
    tiles = SLAB // LANES
    expand = expand.reshape(LANES, 2, tiles, LANES).transpose(0, 2, 1, 3).reshape(LANES, 2 * SLAB)
    reduce = reduce.reshape(2, tiles, LANES, LANES).transpose(1, 0, 2, 3).reshape(2 * SLAB, LANES)
    slots = np.zeros((count // AT, count), np.float32)
    z, y, x, a = np.meshgrid(
        np.arange(size_z), np.arange(size_y), np.arange(size_x), np.arange(AT), indexing="ij"
    )
    slots[((z * size_x + x) * size_y + y).reshape(-1), where.reshape(-1)] = 1.0
    kind = jnp.bfloat16
    return (
        perm.reshape(9 * count, count).astype(kind),
        expand.astype(kind),
        reduce.astype(kind),
        slots.astype(kind),
    )


def coarse_solve(rows, rhs, owner):
    size_z = lax.axis_size("gz")
    size_y = lax.axis_size("gy")
    size_x = lax.axis_size("gx")
    count = rows.shape[0]
    perm, expand, reduce, slots = index_tables(size_z, size_y, size_x)
    mine = (owner.reshape(1, -1) == lax.axis_index(("gz", "gx"))).astype(jnp.bfloat16)
    pick = slots * mine
    padded = jnp.pad(rhs.astype(jnp.float32), ((0, 0), (0, LANES - 2 * NV)))
    return pl.pallas_call(
        gmres_kernel,
        out_shape=(
            jax.ShapeDtypeStruct((count // AT, 9 * SLAB), jnp.bfloat16),
            jax.ShapeDtypeStruct((count // AT, LANES), jnp.float32),
        ),
        in_specs=[pl.BlockSpec(memory_space=pltpu.VMEM)] * 6,
        out_specs=[pl.BlockSpec(memory_space=pltpu.VMEM)] * 2,
        scratch_shapes=[
            pltpu.VMEM((9 * count, LANES), jnp.bfloat16),
            pltpu.VMEM((count, 2 * SLAB), jnp.float32),
        ],
        compiler_params=pltpu.CompilerParams(vmem_limit_bytes=60 << 20),
    )(rows, padded, perm, expand, reduce, pick)


def on_device(vectors, links, site_term, owner, coarse_rhs):
    local_vec = vectors[0, 0, 0]
    local_link = links[0, 0, 0]
    local_site = site_term[0, 0, 0]
    blocks = fine_blocks(local_vec, local_link, local_site)
    rows_flat = blocks.astype(jnp.bfloat16).reshape(blocks.shape[0], -1)
    rhs_flat = coarse_rhs[0, 0, 0].reshape(blocks.shape[0], -1)
    everyone = ("gz", "gy", "gx")
    rows = lax.all_gather(rows_flat, everyone, axis=0, tiled=True)
    rhs = lax.all_gather(rhs_flat, everyone, axis=0, tiled=True)
    operator, answer = coarse_solve(rows, rhs, owner)
    slots = operator.shape[0]
    return (
        operator.reshape(1, slots, 9, 2, NV * NV),
        answer[:, : 2 * NV].reshape(1, slots, 2, NV),
    )


def solution(mesh):
    return jax.shard_map(
        on_device,
        mesh=mesh,
        in_specs=(
            P("gz", "gy", "gx", None, None, None, None, None, None),
            P("gz", "gy", "gx", None, None, None, None, None, None),
            P("gz", "gy", "gx", None, None, None, None, None, None),
            P(),
            P("gz", "gy", "gx", None, None, None),
        ),
        out_specs=(P(("gz", "gx"), None, None, None, None), P(("gz", "gx"), None, None, None)),
        check_vma=False,
    )
```

profile of v0, /device:TPU:0, one launch (start us, length us, event | category | flops | bytes accessed | tf_op | source)
XLA Modules:
  0.0 168.4 jit_solution(2397950022879242471)
XLA Ops:
  7.2 0.0 copy-start.4
  7.2 0.0 all-gather.4.cloned.1.call-start
  7.2 1.5 copy.30
  8.8 0.0 copy-done.4
  8.8 0.0 copy-start
  8.8 0.1 copy.31
  8.9 0.1 copy.34.link_ref
  8.9 3.2 %shard_map.104 = (bf16[4,4,12,24,256]{4,3,2,1,0:T(8,128)(2,1)S(1)}, bf16[4,4,12,24,256]{4,3,2,1,0:T(8,128)(2,1)S(1)}) custom-call(bf16[4,24,24,256]{3,2,1,0:T(8,128)(2,1)S(1)} %bitcast.44, f32[4,72,256]{2,1,0:T(8,128)S(1)} %copy.34.link_ref), custom_call_target="tpu_custom_call" | custom-call | tf_op jit(solution)/shard_map/pallas_call | solution.py:203
  12.1 0.0 copy-start.1
  12.2 0.0 copy-start.2
  12.2 0.1 slice_bitcast_fusion.3
  12.3 0.0 copy-done
  12.3 0.0 copy-start.3
  12.3 5.1 %collective-permute-start = (bf16[4,12,24,256]{3,2,1,0:T(8,128)(2,1)S(1)}, bf16[4,12,24,256]{3,2,1,0:T(8,128)(2,1)S(1)}, u32[]{:S(2)}, u32[]{:S(2)}) collective-permute-start(bf16[4,12,24,256]{3,2,1,0:T(8,128)(2,1)S(1)} %get-tuple-element.20), channel_id=1, source_target_pairs={{1,0},{2,1},{3,2},{0,3},{5,4},{6,5},{7,6},{4,7},{9,8},{10,9},{11,1... | collective-permute-start | bytes 1769480 | tf_op jit(solution)/shard_map/ppermute | solution.py:44
  17.4 0.0 collective-permute-start.1
  17.4 2.4 %collective-permute-start.2 = (bf16[4,12,24,256]{3,2,1,0:T(8,128)(2,1)S(1)}, bf16[4,12,24,256]{3,2,1,0:T(8,128)(2,1)S(1)}, u32[]{:S(2)}, u32[]{:S(2)}) collective-permute-start(bf16[4,12,24,256]{3,2,1,0:T(8,128)(2,1)S(1)} %get-tuple-element.18), channel_id=1, source_target_pairs={{8,0},{16,8},{24,16},{0,24},{9,1},{17,9},{25,17},{1,25},{10,2},{18... | collective-permute-start | bytes 1769480 | tf_op jit(solution)/shard_map/ppermute | solution.py:44
  19.9 0.1 slice_bitcast_fusion
  20.0 0.1 collective-permute-start.3
  20.1 0.3 collective-permute-start.4
  20.4 10.8 %collective-permute-done.rest_0_ = bf16[4,12,24,256]{3,2,1,0:T(8,128)(2,1)S(1)} collective-permute-done((bf16[4,12,24,256]{3,2,1,0:T(8,128)(2,1)S(1)}, bf16[4,12,24,256]{3,2,1,0:T(8,128)(2,1)S(1)}, u32[]{:S(2)}, u32[]{:S(2)}) %collective-permute-start) | collective-permute-done | bytes 589856 | tf_op jit(solution)/shard_map/ppermute | solution.py:44
  31.2 1.5 collective-permute-start.5
  32.7 0.0 copy-done.3
  32.7 0.2 copy.32
  32.9 0.1 copy.35.site_ref
  33.0 0.0 copy-done.1
  33.0 0.0 copy-done.2
  33.0 0.1 slice_bitcast_fusion.6
  33.1 0.1 pad_maximum_fusion.2.rest_7_
  33.1 0.1 pad_maximum_fusion.1.rest_3_
  33.2 0.0 collective-permute-done.1.rest_1_
  33.2 0.5 collective-permute-done.2.rest_2_
  33.6 9.9 %collective-permute-done.3.rest_4_ = bf16[4,12,24,256]{3,2,1,0:T(8,128)(2,1)S(1)} collective-permute-done((bf16[4,12,24,256]{3,2,1,0:T(8,128)(2,1)S(1)}, bf16[4,12,24,256]{3,2,1,0:T(8,128)(2,1)S(1)}, u32[]{:S(2)}, u32[]{:S(2)}) %collective-permute-start.3) | collective-permute-done | bytes 589856 | tf_op jit(solution)/shard_map/ppermute | solution.py:44
  43.6 0.0 collective-permute-done.4.rest_5_
  43.6 3.2 %collective-permute-done.5.rest_6_ = bf16[4,12,24,256]{3,2,1,0:T(8,128)(2,1)S(1)} collective-permute-done((bf16[4,12,24,256]{3,2,1,0:T(8,128)(2,1)S(1)}, bf16[4,12,24,256]{3,2,1,0:T(8,128)(2,1)S(1)}, u32[]{:S(2)}, u32[]{:S(2)}) %collective-permute-start.5) | collective-permute-done | bytes 589856 | tf_op jit(solution)/shard_map/ppermute | solution.py:44
  46.8 10.3 %shard_map.105 = f32[4,9,48,96]{3,2,1,0:T(8,128)} custom-call(bf16[4,24,24,256]{3,2,1,0:T(8,128)(2,1)} %bitcast.45, f32[4,72,256]{2,1,0:T(8,128)S(1)} %copy.34.link_ref, f32[4,144,256]{2,1,0:T(8,128)S(1)} %copy.35.site_ref, bf16[4,4,12,24,256]{4,3,2,1,0:T(8,128)(2,1)} %copy-done.1, bf16[4,4,12,24,256]{4,3,2,1,0:T(8,128)(2,1)} %copy-done.2, ...), custom_call_target="tpu_custom_call" | custom-call | tf_op jit(solution)/shard_map/pallas_call | solution.py:216
  57.1 4.3 %reshape.92 = f32[4,9,2,24,2,2,24]{6,5,4,3,2,1,0:T(2,128)S(1)} reshape(f32[4,9,48,96]{3,2,1,0:T(8,128)} %shard_map.105) | data formatting | bytes 1327104 | tf_op jit(solution)/shard_map/reshape | solution.py:224
  61.4 2.3 %fusion.4 = (f32[4,9,1,24,2,1,24]{6,5,4,3,2,1,0:T(1,128)S(1)}, f32[4,9,1,24,2,1,24]{6,5,4,3,2,1,0:T(1,128)S(1)}, f32[4,9,1,24,2,1,24]{6,5,4,3,2,1,0:T(1,128)S(1)}) fusion(f32[4,9,2,24,2,2,24]{6,5,4,3,2,1,0:T(2,128)S(1)} %reshape.92), kind=kLoop, calls=%fused_computation.28 | loop fusion | flops 41472 | bytes 1161216 | tf_op jit(solution)/shard_map/slice | solution.py:225
  63.8 0.5 add_bitcast_fusion
  64.2 1.6 fusion
  65.8 0.0 copy-start.5
  65.8 0.0 copy-start.7
  65.8 0.0 copy-start.6
  65.8 0.1 slice_reduce_fusion
  65.9 0.1 fusion.1
  66.0 0.1 pad_maximum_fusion.3
  66.2 1.1 reshape.98
  67.3 0.0 all-gather.4.cloned.1.call-update
  67.3 0.0 copy-done.5
  67.4 0.1 reshape.97
  67.5 0.0 copy-done.7
  67.5 0.1 reshape.100
  67.6 65.1 %all-gather.1 = bf16[32,4,48]{2,1,0:T(4,128)(2,1)S(1)} all-gather(bf16[1,4,48]{2,1,0:T(4,128)(2,1)S(1)} %reshape.100), channel_id=1, replica_groups=mesh['gz'=4,'gy'=2,'gx'=4] {'gz','gy','gx'}, dimensions={0}, use_global_device_ids=true | all-gather | bytes 12672 | tf_op jit(solution)/shard_map/all_gather | solution.py:454
  132.6 0.6 pad_convert_fusion.rhs_ref
  133.3 0.0 copy-done.6
  133.3 0.6 broadcast_multiply_fusion.pick_ref
  133.9 0.0 all-gather.4.cloned.1.call-done
  133.9 4.2 %reshape.99.rows_ref = bf16[128,10368]{1,0:T(8,128)(2,1)} reshape(bf16[32,4,10368]{2,1,0:T(4,128)(2,1)} %all-gather.4.cloned.1.call-done) | data formatting | bytes 5308416
  138.1 19.1 %shard_map.106 = (bf16[32,10368]{1,0:T(8,128)(2,1)}, f32[32,128]{1,0:T(8,128)}) custom-call(bf16[128,10368]{1,0:T(8,128)(2,1)} %reshape.99.rows_ref, f32[128,128]{1,0:T(8,128)} %pad_convert_fusion.rhs_ref, bf16[1152,128]{1,0:T(8,128)(2,1)} %constant.30.clone.perm_ref, bf16[128,2304]{1,0:T(8,128)(2,1)} %constant.31.clone.expand_ref, ...), custom_call_target="tpu_custom_call" | custom-call | tf_op jit(solution)/shard_map/pallas_call | solution.py:429
  157.2 3.0 %reshape.93 = bf16[1,32,9,2,576]{4,3,2,1,0:T(2,128)(2,1)} reshape(bf16[32,10368]{1,0:T(8,128)(2,1)} %get-tuple-element.8) | data formatting | bytes 1327104 | tf_op jit(solution)/shard_map/reshape | solution.py:458
  160.2 1.4 copy.40
  (4 shorter events, 0.1 us)
Async XLA Ops:
  7.2 1.6 copy-start.4
  7.2 126.7 %all-gather.4.cloned.1.call-start = ((), (), s32[]{:S(2)}) async-start(), calls=%async_computation | async-start | bytes 2737152 | tf_op jit(solution)/shard_map/all_gather | solution.py:453
  8.8 3.5 %copy-start = (bf16[4,2,4,3,24,256]{5,4,3,2,1,0:T(8,128)(2,1)}, bf16[4,2,4,3,24,256]{5,4,3,2,1,0:T(8,128)(2,1)S(1)}, u32[]{:S(2)}) copy-start(bf16[4,2,4,3,24,256]{5,4,3,2,1,0:T(8,128)(2,1)S(1)} %copy.30) | copy-start | bytes 3538948
  12.1 20.8 %copy-start.1 = (bf16[4,4,12,24,256]{4,3,2,1,0:T(8,128)(2,1)}, bf16[4,4,12,24,256]{4,3,2,1,0:T(8,128)(2,1)S(1)}, u32[]{:S(2)}) copy-start(bf16[4,4,12,24,256]{4,3,2,1,0:T(8,128)(2,1)S(1)} %get-tuple-element.6.minus_ref) | copy-start | bytes 7077892
  12.2 20.8 %copy-start.2 = (bf16[4,4,12,24,256]{4,3,2,1,0:T(8,128)(2,1)}, bf16[4,4,12,24,256]{4,3,2,1,0:T(8,128)(2,1)S(1)}, u32[]{:S(2)}) copy-start(bf16[4,4,12,24,256]{4,3,2,1,0:T(8,128)(2,1)S(1)} %get-tuple-element.7.back_ref) | copy-start | bytes 7077892
  12.3 20.4 %copy-start.3 = (bf16[1,1,1,4,2,2,6,6,256]{8,5,7,6,4,3,2,1,0:T(2,128)(2,1)S(1)}, bf16[1,1,1,4,2,2,6,6,256]{8,5,7,6,4,3,2,1,0:T(2,128)(2,1)}, u32[]{:S(2)}) copy-start(bf16[1,1,1,4,2,2,6,6,256]{8,5,7,6,4,3,2,1,0:T(2,128)(2,1)} %param.11) | copy-start | bytes 884740
  12.3 18.9 %collective-permute-start = (bf16[4,12,24,256]{3,2,1,0:T(8,128)(2,1)S(1)}, bf16[4,12,24,256]{3,2,1,0:T(8,128)(2,1)S(1)}, u32[]{:S(2)}, u32[]{:S(2)}) collective-permute-start(bf16[4,12,24,256]{3,2,1,0:T(8,128)(2,1)S(1)} %get-tuple-element.20), channel_id=1, source_target_pairs={{1,0},{2,1},{3,2},{0,3},{5,4},{6,5},{7,6},{4,7},{9,8},{10,9},{11,1... | collective-permute-start | bytes 1769480 | tf_op jit(solution)/shard_map/ppermute | solution.py:44
  17.4 15.7 %collective-permute-start.1 = (bf16[4,12,24,256]{3,2,1,0:T(8,128)(2,1)S(1)}, bf16[4,12,24,256]{3,2,1,0:T(8,128)(2,1)S(1)}, u32[]{:S(2)}, u32[]{:S(2)}) collective-permute-start(bf16[4,12,24,256]{3,2,1,0:T(8,128)(2,1)S(1)} %get-tuple-element.19), channel_id=1, source_target_pairs={{4,0},{0,4},{5,1},{1,5},{6,2},{2,6},{7,3},{3,7},{12,8},{8,12},{13,... | collective-permute-start | bytes 1769480 | tf_op jit(solution)/shard_map/ppermute | solution.py:44
  17.4 16.2 %collective-permute-start.2 = (bf16[4,12,24,256]{3,2,1,0:T(8,128)(2,1)S(1)}, bf16[4,12,24,256]{3,2,1,0:T(8,128)(2,1)S(1)}, u32[]{:S(2)}, u32[]{:S(2)}) collective-permute-start(bf16[4,12,24,256]{3,2,1,0:T(8,128)(2,1)S(1)} %get-tuple-element.18), channel_id=1, source_target_pairs={{8,0},{16,8},{24,16},{0,24},{9,1},{17,9},{25,17},{1,25},{10,2},{18... | collective-permute-start | bytes 1769480 | tf_op jit(solution)/shard_map/ppermute | solution.py:44
  20.0 23.6 %collective-permute-start.3 = (bf16[4,12,24,256]{3,2,1,0:T(8,128)(2,1)S(1)}, bf16[4,12,24,256]{3,2,1,0:T(8,128)(2,1)S(1)}, u32[]{:S(2)}, u32[]{:S(2)}) collective-permute-start(bf16[4,12,24,256]{3,2,1,0:T(8,128)(2,1)S(1)} %get-tuple-element.17), channel_id=1, source_target_pairs={{3,0},{0,1},{1,2},{2,3},{7,4},{4,5},{5,6},{6,7},{11,8},{8,9},{9,10... | collective-permute-start | bytes 1769480 | tf_op jit(solution)/shard_map/ppermute | solution.py:44
  20.1 23.5 %collective-permute-start.4 = (bf16[4,12,24,256]{3,2,1,0:T(8,128)(2,1)S(1)}, bf16[4,12,24,256]{3,2,1,0:T(8,128)(2,1)S(1)}, u32[]{:S(2)}, u32[]{:S(2)}) collective-permute-start(bf16[4,12,24,256]{3,2,1,0:T(8,128)(2,1)S(1)} %get-tuple-element.16), channel_id=1, source_target_pairs={{4,0},{0,4},{5,1},{1,5},{6,2},{2,6},{7,3},{3,7},{12,8},{8,12},{13,... | collective-permute-start | bytes 1769480 | tf_op jit(solution)/shard_map/ppermute | solution.py:44
  31.2 15.6 %collective-permute-start.5 = (bf16[4,12,24,256]{3,2,1,0:T(8,128)(2,1)S(1)}, bf16[4,12,24,256]{3,2,1,0:T(8,128)(2,1)S(1)}, u32[]{:S(2)}, u32[]{:S(2)}) collective-permute-start(bf16[4,12,24,256]{3,2,1,0:T(8,128)(2,1)S(1)} %get-tuple-element.15), channel_id=1, source_target_pairs={{24,0},{0,8},{8,16},{16,24},{25,1},{1,9},{9,17},{17,25},{26,2},{2,... | collective-permute-start | bytes 1769480 | tf_op jit(solution)/shard_map/ppermute | solution.py:44
  65.8 1.5 copy-start.5
  65.8 1.6 copy-start.7
  65.8 67.4 %copy-start.6 = (bf16[32,128]{1,0:T(8,128)(2,1)S(1)}, bf16[32,128]{1,0:T(8,128)(2,1)}, u32[]{:S(2)}) copy-start(bf16[32,128]{1,0:T(8,128)(2,1)} %constant.29.clone) | copy-start | bytes 24580
Sparse Core Ops, SparseCore 0:
  67.4 57.4 all-gather.3
where the time goes:
time: 169 us; the launch traced here: 168 us
  blocking collectives  65.1 us (39%)
  Pallas kernels  32.6 us (19%)
  waiting for transfers between devices  24.4 us (14%)
  local copies, waits for them, and re-layouts  16.6 us (10%)
  between operations  14.3 us (8%)
  starting transfers between devices  9.42 us (6%)
  other arithmetic  5.95 us (4%)
    all_gather x1, blocking collectives, on_device(): rhs = lax.all_gather(rhs_flat, everyone, axis=0, tiled=True)  65.1 us
    ppermute x6, waiting for transfers between devices, from_behind(): return lax.ppermute(block, axis, route)  24.4 us
    pallas_call x1, Pallas kernels, coarse_solve(): pl.pallas_call(gmres_kernel, out_shape=(jax.ShapeDtypeStruct((count // AT...  19.1 us
    pallas_call x1, Pallas kernels, fine_blocks(): pl.pallas_call(restrict_kernel, grid=(AT,), in_specs=[vec_spec, link_spec...  10.3 us
    ppermute x6, starting transfers between devices, from_behind(): return lax.ppermute(block, axis, route)  9.38 us
    unnamed x19, local copies, waits for them, and re-layouts  5.5 us
    reshape x1, local copies, waits for them, and re-layouts, fine_blocks(): parts = products.reshape(AT, 9, 2, NV, 2, 2, NV)  4.3 us
  transfers between devices with their start and end apart: 7, of which 4 were waited for; matrix products, arithmetic and copies ran while one was open for 1% of the time, Pallas kernels for 0%

commit v1 on v0

--- a/solution.py
+++ b/solution.py
@@ -11,7 +11,12 @@
 ITERS = 4
 PAIR = 1
 LANES = 128
-SLAB = 2 * NV * NV
+GROUP = LANES // NV
+CHUNKS = -(-NV // GROUP)
+ROWS = 2 * AT
+TILES = 9 * CHUNKS
+WIDE = (TILES + 1) * LANES
+MESH = pl.DeviceIdType.MESH
 
 
 coarse_scale = 1.0 / 256.0
@@ -97,9 +102,36 @@
     return jnp.concatenate(pieces, axis=0).astype(jnp.bfloat16)
 
 
-def restrict_kernel(vec_ref, link_ref, site_ref, minus_ref, back_ref, *rest):
-    near_minus, near_back, out_ref = rest[0:4], rest[4:8], rest[8]
+def merged(product):
+    lane = lax.broadcasted_iota(jnp.int32, (NV, LANES), 1)
+    wide = jnp.concatenate([product, jnp.zeros((2 * NV, LANES - 4 * NV), jnp.float32)], axis=1)
+    low = wide[NV:]
+    crossed = jnp.where(
+        lane // NV % 2 == 0, pltpu.roll(low, LANES - NV, 1), -pltpu.roll(low, NV, 1)
+    )
+    return wide[:NV] + crossed
+
+
+def restrict_kernel(vec_ref, link_ref, site_ref, rhs_ref, minus_ref, back_ref, *rest):
+    near_minus, near_back = rest[0:4], rest[4:8]
+    msg_ref, block_ref, flat_ref = rest[8:]
+    step = pl.program_id(0)
     sites = vec_ref.shape[-1]
+    lane8 = lax.broadcasted_iota(jnp.int32, (8, LANES), 1)
+    block_ref[NV:] = jnp.zeros((block_ref.shape[0] - NV, LANES), jnp.float32)
+
+    def emit(k, block):
+        block_ref[:NV] = rounded(block)
+        pieces = [jnp.zeros((8, LANES), jnp.float32)] * 2
+        for at in range(GROUP):
+            rows = block_ref[pl.ds(at, 8, stride=GROUP), :]
+            for part in range(2):
+                shift = (at - part) * NV % LANES
+                moved = rows if shift == 0 else pltpu.roll(rows, shift, 1)
+                pieces[part] = jnp.where(lane8 // NV == at, moved, pieces[part])
+        for part in range(2):
+            flat_ref[k, pl.ds(pl.multiple_of(step * 16 + part * 8, 8), 8), :] = pieces[part]
+
     left, right = [], []
     for chirality in range(2):
         for i in range(6):
@@ -117,7 +149,7 @@
             left.append(
                 stacked([vec_ref[0, at].astype(jnp.float32), vec_ref[0, 12 + at].astype(jnp.float32)])
             )
-    out_ref[0, 0] = contract(left, right)
+    own = merged(contract(left, right))
     position = lax.broadcasted_iota(jnp.int32, (NV, sites), 1)
     for mu in range(4):
         stride = site_strides[mu]
@@ -168,7 +200,9 @@
                 left.append(
                     stacked([minus_ref[mu, 0, part * 6 + at].astype(jnp.float32) for part in range(2)])
                 )
-        out_ref[0, 2 * mu + 1] = contract(left, right)
+        both = merged(contract(left, right))
+        own = own - 0.5 * both
+        emit(2 * mu + 1, pltpu.roll(both, LANES - 2 * NV, 1) * (-0.5 * coarse_scale))
         left, right = [], []
         for spin in range(2):
             for col in range(3):
@@ -185,17 +219,34 @@
                 ]
                 right.append(split(pair, first))
                 left.append(stacked(half(vec_ref, mu, spin, col, 1)))
-        out_ref[0, 2 * mu + 2] = contract(left, right)
-
-
-def fine_blocks(vectors, links, site_term):
+        both = merged(contract(left, right))
+        own = own - 0.5 * both
+        emit(2 * mu + 2, pltpu.roll(both, LANES - 2 * NV, 1) * (-0.5 * coarse_scale))
+    emit(0, own * coarse_scale)
+
+    @pl.when(step == AT - 1)
+    def _():
+        for k in range(9):
+            for chunk in range(CHUNKS):
+                at = (k * CHUNKS + chunk) * LANES
+                msg_ref[:, at : at + LANES] = flat_ref[
+                    k, pl.ds(chunk, ROWS, stride=8), :
+                ].astype(jnp.bfloat16)
+        msg_ref[:, TILES * LANES :] = rhs_ref[...]
+
+
+def fine_message(vectors, links, site_term, rhs):
     sites = vectors.shape[-1]
     vec = jnp.transpose(vectors, (0, 2, 3, 4, 1, 5)).reshape(AT, 24, NV, sites)
     link_f = links.astype(jnp.float32).reshape(AT, 72, sites)
     site_f = site_term.astype(jnp.float32).reshape(AT, 144, sites)
+    tiled = jnp.concatenate(
+        [rhs.reshape(ROWS, NV)] * GROUP + [jnp.zeros((ROWS, LANES - GROUP * NV), rhs.dtype)], axis=1
+    )
     vec_spec = pl.BlockSpec((1, 24, NV, sites), lambda a: (a, 0, 0, 0))
     link_spec = pl.BlockSpec((1, 72, sites), lambda a: (a, 0, 0))
     site_spec = pl.BlockSpec((1, 144, sites), lambda a: (a, 0, 0))
+    rhs_spec = pl.BlockSpec((ROWS, LANES), lambda a: (0, 0))
     half_spec = pl.BlockSpec((4, 1, 12, NV, sites), lambda a: (0, a, 0, 0, 0))
     near_spec = pl.BlockSpec((1, 12, NV, sites), lambda a: (a, 0, 0, 0))
     half_shape = jax.ShapeDtypeStruct((4, AT, 12, NV, sites), jnp.bfloat16)
@@ -213,21 +264,18 @@
     near_back = [from_behind(back[mu], axes[mu], 1) for mu in range(3)]
     near_minus.append(jnp.roll(minus[3], -1, axis=0))
     near_back.append(jnp.roll(back[3], 1, axis=0))
-    products = pl.pallas_call(
+    return pl.pallas_call(
         restrict_kernel,
         grid=(AT,),
-        in_specs=[vec_spec, link_spec, site_spec, half_spec, half_spec] + [near_spec] * 8,
-        out_specs=pl.BlockSpec((1, 9, 2 * NV, 4 * NV), lambda a: (a, 0, 0, 0)),
-        out_shape=jax.ShapeDtypeStruct((AT, 9, 2 * NV, 4 * NV), jnp.float32),
+        in_specs=[vec_spec, link_spec, site_spec, rhs_spec, half_spec, half_spec] + [near_spec] * 8,
+        out_specs=pl.BlockSpec((ROWS, WIDE), lambda a: (0, 0)),
+        out_shape=jax.ShapeDtypeStruct((ROWS, WIDE), jnp.bfloat16),
+        scratch_shapes=[
+            pltpu.VMEM((8 * GROUP, LANES), jnp.float32),
+            pltpu.VMEM((9, 8 * ROWS, LANES), jnp.float32),
+        ],
         compiler_params=params,
-    )(vec, link_f, site_f, minus, back, *near_minus, *near_back)
-    parts = products.reshape(AT, 9, 2, NV, 2, 2, NV)
-    real = parts[:, :, 0, :, :, 0] + parts[:, :, 1, :, :, 1]
-    imag = parts[:, :, 0, :, :, 1] - parts[:, :, 1, :, :, 0]
-    both = jnp.stack([real, imag], 2)
-    inside, outside = both[:, :, :, :, 0], both[:, :, :, :, 1]
-    own = (inside[:, :1] - 0.5 * jnp.sum(inside[:, 1:], axis=1, keepdims=True)) * coarse_scale
-    return jnp.concatenate([own, outside[:, 1:] * (-0.5 * coarse_scale)], axis=1)
+    )(vec, link_f, site_f, tiled, minus, back, *near_minus, *near_back)
 
 
 def complex_mul(first, second):
@@ -303,161 +351,381 @@
     return high, low
 
 
-def turn(value):
-    lane = lax.broadcasted_iota(jnp.int32, value.shape, 1)
-    down = pltpu.roll(value, LANES - NV, 1)
-    up = pltpu.roll(value, NV, 1)
-    return jnp.where(lane < NV, down, jnp.where(lane < 2 * NV, -up, 0.0))
+def gather_kernel(msg_ref, out_ref, chain_sem, plane_sem, cross_sem, core_sem, recv_sem, own_sem):
+    size_z, size_y, size_x = (lax.axis_size(name) for name in ("gz", "gy", "gx"))
+    z, y, x = (lax.axis_index(name) for name in ("gz", "gy", "gx"))
+    middle = TILES // 2 * LANES
+    spans = (pl.ds(0, middle), pl.ds(middle, WIDE - middle))
+
+    def flipped(bits):
+        low, high = z % 2, z // 2
+        if bits & 1:
+            low = 1 - low
+        if bits & 2:
+            high = 1 - high
+        return high * 2 + low
+
+    def slot(at_z, at_y, at_x):
+        return (at_z * size_y + at_y) * size_x + at_x
+
+    def copy(source, at, part, sem, target):
+        return pltpu.make_async_remote_copy(
+            src_ref=source.at[:, spans[part]],
+            dst_ref=out_ref.at[at, :, spans[part]],
+            send_sem=sem,
+            recv_sem=recv_sem.at[at, part],
+            device_id=target,
+            device_id_type=MESH,
+        )
+
+    others = [(y + step) % size_y for step in range(1, size_y)]
+    sides = ((x > 0, x - 1), (x < size_x - 1, x + 1))
+    barrier = pltpu.get_barrier_semaphore()
+    for bits in (1, 2):
+        pl.semaphore_signal(
+            barrier, inc=1, device_id=(flipped(bits), y, x), device_id_type=MESH
+        )
+    for other in others:
+        pl.semaphore_signal(barrier, inc=1, device_id=(z, other, x), device_id_type=MESH)
+    for exists, at in sides:
+
+        @pl.when(exists)
+        def _():
+            pl.semaphore_signal(barrier, inc=1, device_id=(z, y, at), device_id_type=MESH)
+
+    inner = (x > 0).astype(jnp.int32) + (x < size_x - 1).astype(jnp.int32)
+    pl.semaphore_wait(barrier, 1 + size_y + inner)
+
+    mine = slot(z, y, x)
+    keep = pltpu.make_async_copy(msg_ref, out_ref.at[mine], own_sem)
+    keep.start()
+
+    def to_side(source, at_x, side, part):
+        return copy(
+            source, slot(z, y, at_x), part, chain_sem.at[side, at_x, part], (z, y, sides[side][1])
+        )
+
+    def to_plane(source, at_x, which, part):
+        return copy(
+            source,
+            slot(z, y, at_x),
+            part,
+            plane_sem.at[which, at_x, part],
+            (flipped(which + 1), y, x),
+        )
+
+    def to_cross(at_x, which):
+        at = slot(flipped(which + 1), y, at_x)
+        return copy(
+            out_ref.at[at], at, which, cross_sem.at[which, at_x], (flipped(2 - which), y, x)
+        )
+
+    def to_core(source, bits, at_x, which, part):
+        at = slot(flipped(bits), y, at_x)
+        return copy(source, at, part, core_sem.at[which, bits, at_x, part], (z, others[which], x))
+
+    def arrived(at, part):
+        copy(out_ref.at[at], at, part, own_sem, (z, others[0], x)).wait_recv()
+
+    def spread(source, at_x, toward):
+        for part in range(2):
+            for side in toward:
+
+                @pl.when(sides[side][0])
+                def _():
+                    to_side(source, at_x, side, part).start()
+
+            for which in range(2):
+                to_plane(source, at_x, which, part).start()
+            for which in range(len(others)):
+                to_core(source, 0, at_x, which, part).start()
+
+    def column(at_x, toward):
+        at = slot(z, y, at_x)
+        for part in range(2):
+            arrived(at, part)
+        spread(out_ref.at[at], at_x, toward)
+
+    def next_plane(at_x):
+        for which in range(2):
+            at = slot(flipped(which + 1), y, at_x)
+            for part in (which, 1 - which):
+                arrived(at, part)
+                if part == which:
+                    to_cross(at_x, which).start()
+                for other in range(len(others)):
+                    to_core(out_ref.at[at], which + 1, at_x, other, part).start()
+
+    def far_plane(at_x):
+        at = slot(flipped(3), y, at_x)
+        for part in range(2):
+            arrived(at, part)
+            for other in range(len(others)):
+                to_core(out_ref.at[at], 3, at_x, other, part).start()
+
+    def at_distance(distance, action):
+        if distance == 0:
+            action(x, None)
+            return
+
+        @pl.when(x >= distance)
+        def _():
+            action(x - distance, 1)
+
+        @pl.when(x + distance < size_x)
+        def _():
+            action(x + distance, 0)
+
+    spread(msg_ref, x, (0, 1))
+    for distance in range(1, size_x + 2):
+        if distance < size_x:
+            at_distance(distance, lambda at_x, side: column(at_x, (side,)))
+        if distance - 1 < size_x:
+            at_distance(distance - 1, lambda at_x, side: next_plane(at_x))
+        if 0 <= distance - 2 < size_x:
+            at_distance(distance - 2, lambda at_x, side: far_plane(at_x))
+    keep.wait()
+    for at_x in range(size_x):
+        for bits in range(4):
+            for other in others:
+                for part in range(2):
+                    arrived(slot(flipped(bits), other, at_x), part)
+    for at_x in range(size_x):
+        for part in range(2):
+
+            @pl.when((x > 0) & (x <= at_x))
+            def _():
+                to_side(msg_ref, at_x, 0, part).wait_send()
+
+            @pl.when((x < size_x - 1) & (x >= at_x))
+            def _():
+                to_side(msg_ref, at_x, 1, part).wait_send()
+
+            for which in range(2):
+                to_plane(msg_ref, at_x, which, part).wait_send()
+            for bits in range(4):
+                for which in range(len(others)):
+                    to_core(msg_ref, bits, at_x, which, part).wait_send()
+        for which in range(2):
+            to_cross(at_x, which).wait_send()
+
+
+def gather_messages(message):
+    size_z, size_y, size_x = (lax.axis_size(name) for name in ("gz", "gy", "gx"))
+    assert size_z == 4
+    devices = size_z * size_y * size_x
+    dma = pltpu.SemaphoreType.DMA
+    return pl.pallas_call(
+        gather_kernel,
+        out_shape=jax.ShapeDtypeStruct((devices, ROWS, WIDE), jnp.bfloat16),
+        in_specs=[pl.BlockSpec(memory_space=pltpu.VMEM)],
+        out_specs=pl.BlockSpec(memory_space=pltpu.VMEM),
+        scratch_shapes=[
+            dma((2, size_x, 2)),
+            dma((2, size_x, 2)),
+            dma((2, size_x)),
+            dma((size_y - 1, 4, size_x, 2)),
+            dma((devices, 2)),
+            dma,
+        ],
+        compiler_params=pltpu.CompilerParams(
+            collective_id=1, has_side_effects=True, vmem_limit_bytes=48 << 20
+        ),
+    )(message)
 
 
 def total(value):
     return jnp.sum(jnp.sum(value, axis=0, keepdims=True), axis=1, keepdims=True)
 
 
-def gmres_kernel(
-    rows_ref, rhs_ref, perm_ref, expand_ref, reduce_ref, pick_ref, op_ref, sol_ref, near_ref, acc_ref
-):
-    count = rows_ref.shape[0]
-
-    def apply(vector):
-        high, low = split_two(vector)
-        both = high.astype(jnp.float32) + pltpu.roll(low.astype(jnp.float32), 2 * NV, 1)
-        both = both.astype(jnp.bfloat16)
-        near_ref[...] = jnp.dot(
-            perm_ref[...], both, preferred_element_type=jnp.float32
-        ).astype(jnp.bfloat16)
-
-        @pl.loop(0, SLAB // LANES)
-        def _(chunk):
-            at = pl.multiple_of(chunk * LANES, LANES)
-            wide_at = pl.ds(pl.multiple_of(chunk * 2 * LANES, 2 * LANES), 2 * LANES)
-            sums = jnp.zeros((count, 2 * LANES), jnp.float32)
-            for k in range(9):
-                near = near_ref[k * count : (k + 1) * count]
-                rows = rows_ref[:, pl.ds(k * SLAB + at, LANES)].astype(jnp.float32)
-                wide = jnp.dot(
-                    near, expand_ref[:, wide_at], preferred_element_type=jnp.float32
+def paired(value):
+    row = lax.broadcasted_iota(jnp.int32, value.shape, 0)
+    count = value.shape[0]
+    return jnp.where(row % 2 == 0, pltpu.roll(value, count - 1, 0), pltpu.roll(value, 1, 0))
+
+
+def gmres_kernel(sizes, pick_ref, rows_ref, reduce_ref, op_ref, sol_ref, acc_ref, one_ref, two_ref):
+    size_z, size_y, size_x = sizes
+    devices = size_z * size_y * size_x
+    count = devices * ROWS
+    row = lax.broadcasted_iota(jnp.int32, (count, LANES), 0)
+    lane = lax.broadcasted_iota(jnp.int32, (count, LANES), 1)
+    sign = jnp.where(row % 2 == 0, 1.0, -1.0)
+    even8 = lax.broadcasted_iota(jnp.int32, (ROWS, LANES), 0) % 2 == 0
+    lane8 = lax.broadcasted_iota(jnp.int32, (ROWS, LANES), 1)
+    real = lane < NV
+
+    def tile(ref, at):
+        return ref[pl.ds(pl.multiple_of(at * ROWS, ROWS), ROWS), :]
+
+    def apply(vector, swapped):
+        one_ref[...] = vector * sign
+        two_ref[...] = swapped
+
+        @pl.loop(0, devices)
+        def _(at):
+            x = at % size_x
+            y = at // size_x % size_y
+            z = at // (size_x * size_y)
+
+            def slot(at_z, at_y, at_x):
+                return (at_z * size_y + at_y) * size_x + at_x
+
+            places = (
+                slot(z, y, (x + 1) % size_x),
+                slot(z, y, (x + size_x - 1) % size_x),
+                slot(z, (y + 1) % size_y, x),
+                slot(z, (y + size_y - 1) % size_y, x),
+                slot((z + 1) % size_z, y, x),
+                slot((z + size_z - 1) % size_z, y, x),
+            )
+            near = []
+            for ref in (one_ref, two_ref):
+                own = tile(ref, at)
+                near.append(
+                    [own]
+                    + [tile(ref, place) for place in places]
+                    + [pltpu.roll(own, ROWS - 2, 0), pltpu.roll(own, 2, 0)]
                 )
-                sums = sums + jnp.concatenate([rows, rows], axis=1) * wide
-            acc_ref[:, wide_at] = sums
+            for chunk in range(CHUNKS):
+                sums = [0.0, 0.0]
+                for k in range(9):
+                    start = (k * CHUNKS + chunk) * LANES
+                    rows = rows_ref[at, :, start : start + LANES].astype(jnp.float32)
+                    for part in range(2):
+                        sums[part] = sums[part] + rows * near[part][k]
+                acc_ref[
+                    pl.ds(pl.multiple_of(at * ROWS, ROWS), ROWS), chunk * LANES : (chunk + 1) * LANES
+                ] = jnp.where(
+                    even8,
+                    sums[0] + pltpu.roll(sums[0], ROWS - 1, 0),
+                    sums[1] + pltpu.roll(sums[1], 1, 0),
+                )
 
         high, low = split_two(acc_ref[...])
         return jnp.dot(high, reduce_ref[...], preferred_element_type=jnp.float32) + jnp.dot(
             low, reduce_ref[...], preferred_element_type=jnp.float32
         )
 
-    pick = pick_ref[...]
-    for k in range(9):
-        op_ref[:, k * SLAB : (k + 1) * SLAB] = jnp.dot(
-            pick, rows_ref[:, k * SLAB : (k + 1) * SLAB], preferred_element_type=jnp.float32
-        ).astype(jnp.bfloat16)
-    right_side = rhs_ref[...]
+    for z in range(size_z):
+        for y in range(size_y):
+            for x in range(size_x):
+                at = (z * size_y + y) * size_x + x
+                place = (z * size_x + x) * size_y + y
+                chosen = pick_ref[at]
+
+                @pl.when(chosen < 0)
+                def _():
+                    op_ref[place] = jnp.zeros(op_ref.shape[1:], op_ref.dtype)
+
+                @pl.when(chosen >= 0)
+                def _():
+                    shift = (ROWS - 2 * chosen) % ROWS
+                    for k in range(9):
+                        turned = []
+                        for chunk in range(CHUNKS):
+                            start = (k * CHUNKS + chunk) * LANES
+                            rows = rows_ref[at, :, start : start + LANES].astype(jnp.float32)
+                            rows = pltpu.roll(rows, shift, 0)
+                            back = chunk * (LANES - GROUP * NV)
+                            turned.append(rows if back == 0 else pltpu.roll(rows, LANES - back, 1))
+                        for chunk in range(CHUNKS):
+                            start = chunk * LANES
+                            width = min(LANES, NV * NV - start)
+                            value = turned[chunk]
+                            if chunk + 1 < CHUNKS:
+                                cut = GROUP * NV - chunk * (LANES - GROUP * NV)
+                                value = jnp.where(lane8 < cut, value, turned[chunk + 1])
+                            op_ref[place, k, :, start : start + width] = value[:2, :width].astype(
+                                jnp.bfloat16
+                            )
+
+    right_side = rows_ref[:, :, TILES * LANES :].astype(jnp.float32).reshape(count, LANES)
     zero_value = jnp.zeros((1, 1), jnp.float32)
-    beta = jnp.sqrt(total(right_side * right_side) + epsilon)
+
+    def squares(value):
+        return total(jnp.where(real, value * value, 0.0))
+
+    beta = jnp.sqrt(squares(right_side) + epsilon)
     basis = [right_side / beta]
-    turned = [turn(basis[0])]
+    swapped = [paired(basis[0])]
     hessen = []
     for row_index in range(ITERS + 1):
         hessen.append([(zero_value, zero_value)] * ITERS)
     for column in range(ITERS):
-        work = apply(basis[column])
+        work = apply(basis[column], swapped[column])
         for row_index in range(column + 1):
-            coef_re = total(basis[row_index] * work)
-            coef_im = -total(turned[row_index] * work)
+            turned = swapped[row_index] * sign
+            coef_re = total(jnp.where(real, basis[row_index] * work, 0.0))
+            coef_im = -total(jnp.where(real, turned * work, 0.0))
             hessen[row_index][column] = (coef_re, coef_im)
-            work = work - coef_re * basis[row_index] + coef_im * turned[row_index]
-        norm_now = jnp.sqrt(total(work * work) + epsilon)
+            work = work - coef_re * basis[row_index] + coef_im * turned
+        norm_now = jnp.sqrt(squares(work) + epsilon)
         hessen[column + 1][column] = (norm_now, zero_value)
         if column + 1 < ITERS:
             basis.append(work / norm_now)
-            turned.append(turn(basis[-1]))
+            swapped.append(paired(basis[-1]))
     weights = least_squares(hessen, beta)
     answer = jnp.zeros_like(right_side)
     for column in range(ITERS):
-        answer = answer + weights[column][0] * basis[column] - weights[column][1] * turned[column]
-    high, low = split_two(answer)
-    rest = (answer - high.astype(jnp.float32) - low.astype(jnp.float32)).astype(jnp.bfloat16)
-    sol_ref[...] = (
-        jnp.dot(pick, high, preferred_element_type=jnp.float32)
-        + jnp.dot(pick, low, preferred_element_type=jnp.float32)
-        + jnp.dot(pick, rest, preferred_element_type=jnp.float32)
-    )
-
-
-def index_tables(size_z, size_y, size_x):
-    count = size_z * size_y * size_x * AT
-    where = np.arange(count).reshape(size_z, size_y, size_x, AT)
-    perm = np.zeros((9, count, count), np.float32)
-    for k, offset in enumerate(neighbor_offsets):
-        source = np.roll(where, [-step for step in offset], axis=(0, 1, 2, 3)).reshape(-1)
-        perm[k, np.arange(count), source] = 1.0
-    lane = np.arange(SLAB)
-    comp, row, col = lane // (NV * NV), lane // NV % NV, lane % NV
-    expand = np.zeros((LANES, 2, SLAB), np.float32)
-    reduce = np.zeros((2, SLAB, LANES), np.float32)
-    for half in range(2):
-        expand[half * NV + col, half, lane] = 1.0
-        expand[(2 + half) * NV + col, half, lane] = 1.0
-        out = np.where(comp == half, 0, NV) + row
-        reduce[half, lane, out] = np.where((half == 1) & (comp == 1), -1.0, 1.0)
-    tiles = SLAB // LANES
-    expand = expand.reshape(LANES, 2, tiles, LANES).transpose(0, 2, 1, 3).reshape(LANES, 2 * SLAB)
-    reduce = reduce.reshape(2, tiles, LANES, LANES).transpose(1, 0, 2, 3).reshape(2 * SLAB, LANES)
-    slots = np.zeros((count // AT, count), np.float32)
-    z, y, x, a = np.meshgrid(
-        np.arange(size_z), np.arange(size_y), np.arange(size_x), np.arange(AT), indexing="ij"
-    )
-    slots[((z * size_x + x) * size_y + y).reshape(-1), where.reshape(-1)] = 1.0
-    kind = jnp.bfloat16
-    return (
-        perm.reshape(9 * count, count).astype(kind),
-        expand.astype(kind),
-        reduce.astype(kind),
-        slots.astype(kind),
-    )
-
-
-def coarse_solve(rows, rhs, owner):
-    size_z = lax.axis_size("gz")
-    size_y = lax.axis_size("gy")
-    size_x = lax.axis_size("gx")
-    count = rows.shape[0]
-    perm, expand, reduce, slots = index_tables(size_z, size_y, size_x)
-    mine = (owner.reshape(1, -1) == lax.axis_index(("gz", "gx"))).astype(jnp.bfloat16)
-    pick = slots * mine
-    padded = jnp.pad(rhs.astype(jnp.float32), ((0, 0), (0, LANES - 2 * NV)))
+        answer = (
+            answer
+            + weights[column][0] * basis[column]
+            - weights[column][1] * (swapped[column] * sign)
+        )
+    one_ref[...] = answer
+    for z in range(size_z):
+        for y in range(size_y):
+            for x in range(size_x):
+                at = (z * size_y + y) * size_x + x
+                chosen = pick_ref[at]
+                shift = (ROWS - 2 * jnp.maximum(chosen, 0)) % ROWS
+                rows = pltpu.roll(one_ref[at * ROWS : (at + 1) * ROWS], shift, 0)
+                rows = jnp.where(chosen >= 0, rows, 0.0)
+                sol_ref[(z * size_x + x) * size_y + y] = rows[:2, :NV]
+
+
+def reduce_table():
+    table = np.zeros((CHUNKS, LANES, LANES), np.float32)
+    for chunk in range(CHUNKS):
+        for at in range(GROUP):
+            out = chunk * GROUP + at
+            if out < NV:
+                for copy in range(GROUP):
+                    table[chunk, at * NV : (at + 1) * NV, copy * NV + out] = 1.0
+    return table.reshape(CHUNKS * LANES, LANES).astype(jnp.bfloat16)
+
+
+def coarse_solve(rows, owner):
+    sizes = tuple(lax.axis_size(name) for name in ("gz", "gy", "gx"))
+    devices, count = rows.shape[0], rows.shape[0] * ROWS
+    mine = owner.reshape(-1, AT) == lax.axis_index(("gz", "gx"))
+    chosen = jnp.max(jnp.where(mine, jnp.arange(AT, dtype=jnp.int32), -1), axis=1)
+    vmem = pl.BlockSpec(memory_space=pltpu.VMEM)
     return pl.pallas_call(
-        gmres_kernel,
+        lambda *refs: gmres_kernel(sizes, *refs),
         out_shape=(
-            jax.ShapeDtypeStruct((count // AT, 9 * SLAB), jnp.bfloat16),
-            jax.ShapeDtypeStruct((count // AT, LANES), jnp.float32),
+            jax.ShapeDtypeStruct((devices, 9, 2, NV * NV), jnp.bfloat16),
+            jax.ShapeDtypeStruct((devices, 2, NV), jnp.float32),
         ),
-        in_specs=[pl.BlockSpec(memory_space=pltpu.VMEM)] * 6,
-        out_specs=[pl.BlockSpec(memory_space=pltpu.VMEM)] * 2,
+        in_specs=[pl.BlockSpec(memory_space=pltpu.SMEM), vmem, vmem],
+        out_specs=[vmem, vmem],
         scratch_shapes=[
-            pltpu.VMEM((9 * count, LANES), jnp.bfloat16),
-            pltpu.VMEM((count, 2 * SLAB), jnp.float32),
+            pltpu.VMEM((count, CHUNKS * LANES), jnp.float32),
+            pltpu.VMEM((count, LANES), jnp.float32),
+            pltpu.VMEM((count, LANES), jnp.float32),
         ],
         compiler_params=pltpu.CompilerParams(vmem_limit_bytes=60 << 20),
-    )(rows, padded, perm, expand, reduce, pick)
+    )(chosen, rows, reduce_table())
 
 
 def on_device(vectors, links, site_term, owner, coarse_rhs):
-    local_vec = vectors[0, 0, 0]
-    local_link = links[0, 0, 0]
-    local_site = site_term[0, 0, 0]
-    blocks = fine_blocks(local_vec, local_link, local_site)
-    rows_flat = blocks.astype(jnp.bfloat16).reshape(blocks.shape[0], -1)
-    rhs_flat = coarse_rhs[0, 0, 0].reshape(blocks.shape[0], -1)
-    everyone = ("gz", "gy", "gx")
-    rows = lax.all_gather(rows_flat, everyone, axis=0, tiled=True)
-    rhs = lax.all_gather(rhs_flat, everyone, axis=0, tiled=True)
-    operator, answer = coarse_solve(rows, rhs, owner)
-    slots = operator.shape[0]
-    return (
-        operator.reshape(1, slots, 9, 2, NV * NV),
-        answer[:, : 2 * NV].reshape(1, slots, 2, NV),
+    message = fine_message(
+        vectors[0, 0, 0], links[0, 0, 0], site_term[0, 0, 0], coarse_rhs[0, 0, 0]
     )
+    rows = gather_messages(message)
+    operator, answer = coarse_solve(rows, owner)
+    return operator[None], answer[None]
 
 
 def solution(mesh):

time: 169 us -> 94.6 us (0.56)
  blocking collectives: 65.1 us -> 0 us
  Pallas kernels: 32.6 us -> 52.7 us
  between operations: 14.3 us -> 0.79 us
  local copies, waits for them, and re-layouts: 16.6 us -> 10.2 us
  other arithmetic: 5.95 us -> 1.04 us
  waiting for transfers between devices: 24.4 us -> 20.2 us
    all_gather x1 -> x0, blocking collectives: 65.1 us -> none  [on_device(): rhs = lax.all_gather(rhs_flat, everyone, axis=0, tiled=True)]
    pallas_call x3 -> x4, Pallas kernels: 32.6 us -> 52.7 us  [the longest x1 22.6 us: gather_messages(): pl.pallas_call(gather_kernel, out_shape=jax.ShapeDtypeStruct((devices, RO...]
    reshape x2 -> x0, local copies, waits for them, and re-layouts: 7.3 us -> none  [the longest x1 4.3 us: fine_blocks(): parts = products.reshape(AT, 9, 2, NV, 2, 2, NV)]
    ppermute x6, waiting for transfers between devices: 24.4 us -> 20.2 us  [from_behind(): return lax.ppermute(block, axis, route)]
    unnamed x19 -> x15, local copies, waits for them, and re-layouts: 5.5 us -> 3.06 us
    slice x1 -> x0, other arithmetic: 2.33 us -> none  [fine_blocks(): real = parts[:, :, 0, :, :, 0] + parts[:, :, 1, :, :, 1]]
    squeeze x2, local copies, waits for them, and re-layouts: 0.24 us -> 2.56 us  [the longest x1 1.33 us: fine_message(): near_minus = [from_behind(minus[mu], axes[mu], -1) for mu in range(3)]]
  transfers between devices with their start and end apart: 7 -> 6, of which waited for: 4 -> 3; matrix products, arithmetic and copies ran while one was open for 1% -> 6% of each run, Pallas kernels for 0% -> 0%
where the time goes in v1:
time: 94.6 us; the launch traced here: 94.2 us
  Pallas kernels  52.7 us (56%)
  waiting for transfers between devices  20.2 us (21%)
  local copies, waits for them, and re-layouts  10.2 us (11%)
  starting transfers between devices  9.25 us (10%)
  other arithmetic  1.04 us (1%)
    pallas_call x1, Pallas kernels, gather_messages(): pl.pallas_call(gather_kernel, out_shape=jax.ShapeDtypeStruct((devices, RO...  22.6 us
    ppermute x6, waiting for transfers between devices, from_behind(): return lax.ppermute(block, axis, route)  20.2 us
    pallas_call x1, Pallas kernels, coarse_solve(): pl.pallas_call(lambda *refs: gmres_kernel(sizes, *refs), out_shape=(jax.S...  15.8 us
    pallas_call x1, Pallas kernels, fine_message(): pl.pallas_call(restrict_kernel, grid=(AT,), in_specs=[vec_spec, link_spec...  11.1 us
    ppermute x6, starting transfers between devices, from_behind(): return lax.ppermute(block, axis, route)  9.25 us
    pallas_call x1, Pallas kernels, fine_message(): pl.pallas_call(halves_kernel, grid=(AT,), in_specs=[vec_spec, link_spec],...  3.22 us
    unnamed x15, local copies, waits for them, and re-layouts  3.06 us
    slice x2, local copies, waits for them, and re-layouts, fine_message(): near_back.append(jnp.roll(back[3], 1, axis=0))  2 us
  transfers between devices with their start and end apart: 6, of which 3 were waited for; matrix products, arithmetic and copies ran while one was open for 6% of the time, Pallas kernels for 0%

profile of v1, /device:TPU:0, one launch (start us, length us, event | category | flops | bytes accessed | tf_op | source)
XLA Modules:
  0.0 94.2 jit_solution(14026314730532694465)
XLA Ops:
  0.6 0.0 copy-start.5
  0.6 1.5 %copy.12 = bf16[4,2,4,3,24,256]{5,4,3,2,1,0:T(8,128)(2,1)S(1)} copy(bf16[4,2,4,3,24,256]{5,2,3,1,4,0:T(4,128)(2,1)} %bitcast.32) | data formatting | bytes 2359296 | tf_op jit(solution)/shard_map/transpose | solution.py:240
  2.2 0.0 copy-done.5
  2.2 0.0 copy-start.1
  2.2 0.1 copy.13
  2.3 0.1 copy.16.link_ref
  2.3 3.2 %shard_map.77 = (bf16[4,4,12,24,256]{4,3,2,1,0:T(8,128)(2,1)S(1)}, bf16[4,4,12,24,256]{4,3,2,1,0:T(8,128)(2,1)S(1)}) custom-call(bf16[4,24,24,256]{3,2,1,0:T(8,128)(2,1)S(1)} %bitcast.29, f32[4,72,256]{2,1,0:T(8,128)S(1)} %copy.16.link_ref), custom_call_target="tpu_custom_call" | custom-call | tf_op jit(solution)/shard_map/pallas_call | solution.py:254
  5.6 0.0 copy-start.3
  5.6 0.0 copy-start.2
  5.6 1.3 %slice_bitcast_fusion.3 = (bf16[4,12,24,256]{3,2,1,0:T(8,128)(2,1)}, bf16[4,12,24,256]{3,2,1,0:T(8,128)(2,1)}, bf16[4,12,24,256]{3,2,1,0:T(8,128)(2,1)}) fusion(bf16[4,4,12,24,256]{4,3,2,1,0:T(8,128)(2,1)S(1)} %get-tuple-element.6.minus_ref), kind=kLoop, calls=%fused_computation.5 | loop fusion | bytes 3538944 | tf_op jit(solution)/shard_map/squeeze | solution.py:263
  6.9 0.0 copy-done.1
  6.9 0.0 copy-start.4
  6.9 5.1 %collective-permute-start = (bf16[4,12,24,256]{3,2,1,0:T(8,128)(2,1)}, bf16[4,12,24,256]{3,2,1,0:T(8,128)(2,1)}, u32[]{:S(2)}, u32[]{:S(2)}) collective-permute-start(bf16[4,12,24,256]{3,2,1,0:T(8,128)(2,1)} %get-tuple-element.19), channel_id=1, source_target_pairs={{1,0},{2,1},{3,2},{0,3},{5,4},{6,5},{7,6},{4,7},{9,8},{10,9},{11,1... | collective-permute-start | bytes 1769480 | tf_op jit(solution)/shard_map/ppermute | solution.py:49
  12.0 0.0 collective-permute-start.1
  12.0 2.4 %collective-permute-start.2 = (bf16[4,12,24,256]{3,2,1,0:T(8,128)(2,1)}, bf16[4,12,24,256]{3,2,1,0:T(8,128)(2,1)}, u32[]{:S(2)}, u32[]{:S(2)}) collective-permute-start(bf16[4,12,24,256]{3,2,1,0:T(8,128)(2,1)} %get-tuple-element.17), channel_id=1, source_target_pairs={{8,0},{16,8},{24,16},{0,24},{9,1},{17,9},{25,17},{1,25},{10,2},{18... | collective-permute-start | bytes 1769480 | tf_op jit(solution)/shard_map/ppermute | solution.py:49
  14.4 0.0 copy-start.6
  14.5 1.2 %slice_bitcast_fusion = (bf16[4,12,24,256]{3,2,1,0:T(8,128)(2,1)}, bf16[4,12,24,256]{3,2,1,0:T(8,128)(2,1)}, bf16[4,12,24,256]{3,2,1,0:T(8,128)(2,1)}) fusion(bf16[4,4,12,24,256]{4,3,2,1,0:T(8,128)(2,1)S(1)} %get-tuple-element.7.back_ref), kind=kLoop, calls=%fused_computation.2 | loop fusion | bytes 3538944 | tf_op jit(solution)/shard_map/squeeze | solution.py:264
  15.7 0.0 copy-done.3
  15.7 0.0 collective-permute-start.3
  15.7 0.2 collective-permute-start.4
  15.9 0.0 copy-done.4
  15.9 0.2 copy.14
  16.1 0.1 copy.17.site_ref
  16.2 0.9 slice_bitcast_fusion.8
  17.1 8.9 %collective-permute-done.rest_0_ = bf16[4,12,24,256]{3,2,1,0:T(8,128)(2,1)} collective-permute-done((bf16[4,12,24,256]{3,2,1,0:T(8,128)(2,1)}, bf16[4,12,24,256]{3,2,1,0:T(8,128)(2,1)}, u32[]{:S(2)}, u32[]{:S(2)}) %collective-permute-start) | collective-permute-done | bytes 589856 | tf_op jit(solution)/shard_map/ppermute | solution.py:49
  26.1 1.5 %collective-permute-start.5 = (bf16[4,12,24,256]{3,2,1,0:T(8,128)(2,1)}, bf16[4,12,24,256]{3,2,1,0:T(8,128)(2,1)}, u32[]{:S(2)}, u32[]{:S(2)}) collective-permute-start(bf16[4,12,24,256]{3,2,1,0:T(8,128)(2,1)} %get-tuple-element.14), channel_id=1, source_target_pairs={{24,0},{0,8},{8,16},{16,24},{25,1},{1,9},{9,17},{17,25},{26,2},{2,... | collective-permute-start | bytes 1769480 | tf_op jit(solution)/shard_map/ppermute | solution.py:49
  27.6 0.9 select_reduce_fusion
  28.5 0.6 reduce_max.12.refs_0_
  29.1 0.0 copy-done.6
  29.1 0.1 concatenate.11.rhs_ref
  29.2 0.0 copy-done.2
  29.2 1.1 %slice_bitcast_fusion.6 = (bf16[3,12,24,256]{3,2,1,0:T(8,128)(2,1)S(1)}, bf16[3,12,24,256]{3,2,1,0:T(8,128)(2,1)S(1)}) fusion(bf16[4,4,12,24,256]{4,3,2,1,0:T(8,128)(2,1)} %copy-done.3, bf16[4,4,12,24,256]{4,3,2,1,0:T(8,128)(2,1)S(1)} %get-tuple-element.6.minus_ref), kind=kLoop, calls=%fused_computation.8 | loop fusion | bytes 1769472 | tf_op jit(solution)/shard_map/jit(_roll_static)/slice | solution.py:266
  30.3 0.1 pad_maximum_fusion.1.rest_7_
  30.3 0.1 pad_maximum_fusion.rest_3_
  30.4 0.0 collective-permute-done.1.rest_1_
  30.4 0.0 collective-permute-done.2.rest_2_
  30.4 8.0 %collective-permute-done.3.rest_4_ = bf16[4,12,24,256]{3,2,1,0:T(8,128)(2,1)} collective-permute-done((bf16[4,12,24,256]{3,2,1,0:T(8,128)(2,1)}, bf16[4,12,24,256]{3,2,1,0:T(8,128)(2,1)}, u32[]{:S(2)}, u32[]{:S(2)}) %collective-permute-start.3) | collective-permute-done | bytes 589856 | tf_op jit(solution)/shard_map/ppermute | solution.py:49
  38.4 0.0 collective-permute-done.4.rest_5_
  38.5 3.2 %collective-permute-done.5.rest_6_ = bf16[4,12,24,256]{3,2,1,0:T(8,128)(2,1)} collective-permute-done((bf16[4,12,24,256]{3,2,1,0:T(8,128)(2,1)}, bf16[4,12,24,256]{3,2,1,0:T(8,128)(2,1)}, u32[]{:S(2)}, u32[]{:S(2)}) %collective-permute-start.5) | collective-permute-done | bytes 589856 | tf_op jit(solution)/shard_map/ppermute | solution.py:49
  41.7 11.1 %shard_map.78.msg_ref = bf16[8,5888]{1,0:T(8,128)(2,1)S(1)} custom-call(bf16[4,24,24,256]{3,2,1,0:T(8,128)(2,1)} %bitcast.30, f32[4,72,256]{2,1,0:T(8,128)S(1)} %copy.16.link_ref, f32[4,144,256]{2,1,0:T(8,128)S(1)} %copy.17.site_ref, bf16[8,128]{1,0:T(8,128)(2,1)S(1)} %concatenate.11.rhs_ref, bf16[4,4,12,24,256]{4,3,2,1,0:T(8,128)(2,1)} %copy-done.2, ...), custom_call_target="tpu_custom_call" | custom-call | tf_op jit(solution)/shard_map/pallas_call | solution.py:267
  52.7 22.6 %shard_map.79.refs_1_ = bf16[32,8,5888]{2,1,0:T(8,128)(2,1)S(1)} custom-call(bf16[8,5888]{1,0:T(8,128)(2,1)S(1)} %shard_map.78.msg_ref), custom_call_target="tpu_custom_call" | custom-call | tf_op jit(solution)/shard_map/pallas_call | solution.py:518
  75.4 0.0 copy-start
  75.4 1.6 %copy-done = bf16[32,8,5888]{2,1,0:T(8,128)(2,1)} copy-done((bf16[32,8,5888]{2,1,0:T(8,128)(2,1)}, bf16[32,8,5888]{2,1,0:T(8,128)(2,1)S(1)}, u32[]{:S(2)}) %copy-start) | copy-done | bytes 3014680
  77.0 15.8 %shard_map.80 = (bf16[32,9,2,576]{3,2,1,0:T(2,128)(2,1)}, f32[32,2,24]{2,1,0:T(2,128)}) custom-call(s32[32]{0:T(128)} %reduce_max.12.refs_0_, bf16[32,8,5888]{2,1,0:T(8,128)(2,1)} %copy-done, bf16[640,128]{1,0:T(8,128)(2,1)} %constant.17.clone.refs_2_), custom_call_target="tpu_custom_call" | custom-call | tf_op jit(solution)/shard_map/pallas_call | solution.py:705
  92.7 1.4 %copy.18 = f32[1,32,2,24]{1,3,2,0:T(8,128)} copy(f32[1,32,2,24]{3,2,1,0:T(2,128)} %bitcast.39) | data formatting | bytes 12288
  (1 shorter events, 0.0 us)
Async XLA Ops:
  0.6 1.6 %copy-start.5 = (bf16[1,1,1,4,4,2,3,3,256]{8,5,7,6,4,3,2,1,0:T(2,128)(2,1)S(1)}, bf16[1,1,1,4,4,2,3,3,256]{8,5,7,6,4,3,2,1,0:T(2,128)(2,1)}, u32[]{:S(2)}) copy-start(bf16[1,1,1,4,4,2,3,3,256]{8,5,7,6,4,3,2,1,0:T(2,128)(2,1)} %param.7) | copy-start | bytes 442372
  2.2 4.7 %copy-start.1 = (bf16[4,2,4,3,24,256]{5,4,3,2,1,0:T(8,128)(2,1)}, bf16[4,2,4,3,24,256]{5,4,3,2,1,0:T(8,128)(2,1)S(1)}, u32[]{:S(2)}) copy-start(bf16[4,2,4,3,24,256]{5,4,3,2,1,0:T(8,128)(2,1)S(1)} %copy.12) | copy-start | bytes 3538948
  5.6 10.1 %copy-start.3 = (bf16[4,4,12,24,256]{4,3,2,1,0:T(8,128)(2,1)}, bf16[4,4,12,24,256]{4,3,2,1,0:T(8,128)(2,1)S(1)}, u32[]{:S(2)}) copy-start(bf16[4,4,12,24,256]{4,3,2,1,0:T(8,128)(2,1)S(1)} %get-tuple-element.7.back_ref) | copy-start | bytes 7077892
  5.6 23.6 %copy-start.2 = (bf16[4,4,12,24,256]{4,3,2,1,0:T(8,128)(2,1)}, bf16[4,4,12,24,256]{4,3,2,1,0:T(8,128)(2,1)S(1)}, u32[]{:S(2)}) copy-start(bf16[4,4,12,24,256]{4,3,2,1,0:T(8,128)(2,1)S(1)} %get-tuple-element.6.minus_ref) | copy-start | bytes 7077892
  6.9 9.0 %copy-start.4 = (bf16[1,1,1,4,2,2,6,6,256]{8,5,7,6,4,3,2,1,0:T(2,128)(2,1)S(1)}, bf16[1,1,1,4,2,2,6,6,256]{8,5,7,6,4,3,2,1,0:T(2,128)(2,1)}, u32[]{:S(2)}) copy-start(bf16[1,1,1,4,2,2,6,6,256]{8,5,7,6,4,3,2,1,0:T(2,128)(2,1)} %param.8) | copy-start | bytes 884740
  6.9 19.2 %collective-permute-start = (bf16[4,12,24,256]{3,2,1,0:T(8,128)(2,1)}, bf16[4,12,24,256]{3,2,1,0:T(8,128)(2,1)}, u32[]{:S(2)}, u32[]{:S(2)}) collective-permute-start(bf16[4,12,24,256]{3,2,1,0:T(8,128)(2,1)} %get-tuple-element.19), channel_id=1, source_target_pairs={{1,0},{2,1},{3,2},{0,3},{5,4},{6,5},{7,6},{4,7},{9,8},{10,9},{11,1... | collective-permute-start | bytes 1769480 | tf_op jit(solution)/shard_map/ppermute | solution.py:49
  12.0 18.4 %collective-permute-start.1 = (bf16[4,12,24,256]{3,2,1,0:T(8,128)(2,1)}, bf16[4,12,24,256]{3,2,1,0:T(8,128)(2,1)}, u32[]{:S(2)}, u32[]{:S(2)}) collective-permute-start(bf16[4,12,24,256]{3,2,1,0:T(8,128)(2,1)} %get-tuple-element.18), channel_id=1, source_target_pairs={{4,0},{0,4},{5,1},{1,5},{6,2},{2,6},{7,3},{3,7},{12,8},{8,12},{13,... | collective-permute-start | bytes 1769480 | tf_op jit(solution)/shard_map/ppermute | solution.py:49
  12.0 18.4 %collective-permute-start.2 = (bf16[4,12,24,256]{3,2,1,0:T(8,128)(2,1)}, bf16[4,12,24,256]{3,2,1,0:T(8,128)(2,1)}, u32[]{:S(2)}, u32[]{:S(2)}) collective-permute-start(bf16[4,12,24,256]{3,2,1,0:T(8,128)(2,1)} %get-tuple-element.17), channel_id=1, source_target_pairs={{8,0},{16,8},{24,16},{0,24},{9,1},{17,9},{25,17},{1,25},{10,2},{18... | collective-permute-start | bytes 1769480 | tf_op jit(solution)/shard_map/ppermute | solution.py:49
  14.4 14.7 %copy-start.6 = (bf16[1,1,1,4,2,24]{5,4,3,2,1,0:T(2,128)(2,1)S(1)}, bf16[1,1,1,4,2,24]{5,4,3,2,1,0:T(2,128)(2,1)}, u32[]{:S(2)}) copy-start(bf16[1,1,1,4,2,24]{5,4,3,2,1,0:T(2,128)(2,1)} %param.10) | copy-start | bytes 1156
  15.7 22.8 %collective-permute-start.3 = (bf16[4,12,24,256]{3,2,1,0:T(8,128)(2,1)}, bf16[4,12,24,256]{3,2,1,0:T(8,128)(2,1)}, u32[]{:S(2)}, u32[]{:S(2)}) collective-permute-start(bf16[4,12,24,256]{3,2,1,0:T(8,128)(2,1)} %get-tuple-element.16), channel_id=1, source_target_pairs={{3,0},{0,1},{1,2},{2,3},{7,4},{4,5},{5,6},{6,7},{11,8},{8,9},{9,10... | collective-permute-start | bytes 1769480 | tf_op jit(solution)/shard_map/ppermute | solution.py:49
  15.7 22.8 %collective-permute-start.4 = (bf16[4,12,24,256]{3,2,1,0:T(8,128)(2,1)}, bf16[4,12,24,256]{3,2,1,0:T(8,128)(2,1)}, u32[]{:S(2)}, u32[]{:S(2)}) collective-permute-start(bf16[4,12,24,256]{3,2,1,0:T(8,128)(2,1)} %get-tuple-element.15), channel_id=1, source_target_pairs={{4,0},{0,4},{5,1},{1,5},{6,2},{2,6},{7,3},{3,7},{12,8},{8,12},{13,... | collective-permute-start | bytes 1769480 | tf_op jit(solution)/shard_map/ppermute | solution.py:49
  26.1 15.6 %collective-permute-start.5 = (bf16[4,12,24,256]{3,2,1,0:T(8,128)(2,1)}, bf16[4,12,24,256]{3,2,1,0:T(8,128)(2,1)}, u32[]{:S(2)}, u32[]{:S(2)}) collective-permute-start(bf16[4,12,24,256]{3,2,1,0:T(8,128)(2,1)} %get-tuple-element.14), channel_id=1, source_target_pairs={{24,0},{0,8},{8,16},{16,24},{25,1},{1,9},{9,17},{17,25},{26,2},{2,... | collective-permute-start | bytes 1769480 | tf_op jit(solution)/shard_map/ppermute | solution.py:49
  75.4 1.6 %copy-start = (bf16[32,8,5888]{2,1,0:T(8,128)(2,1)}, bf16[32,8,5888]{2,1,0:T(8,128)(2,1)S(1)}, u32[]{:S(2)}) copy-start(bf16[32,8,5888]{2,1,0:T(8,128)(2,1)S(1)} %shard_map.79.refs_1_) | copy-start | bytes 9043972

commit v2 on v1

--- a/solution.py
+++ b/solution.py
@@ -22,19 +22,6 @@
 coarse_scale = 1.0 / 256.0
 epsilon = 1e-06
 site_strides = (64, 16, 4, 1)
-neighbor_offsets = (
-    (0, 0, 0, 0),
-    (0, 0, 1, 0),
-    (0, 0, -1, 0),
-    (0, 1, 0, 0),
-    (0, -1, 0, 0),
-    (1, 0, 0, 0),
-    (-1, 0, 0, 0),
-    (0, 0, 0, 1),
-    (0, 0, 0, -1),
-)
-
-
 lower_table = (
     (((1, 3, 1), (0, 3, -1)), ((1, 2, 1), (0, 2, -1))),
     (((0, 3, -1), (1, 3, -1)), ((0, 2, 1), (1, 2, 1))),
@@ -43,196 +30,251 @@
 )
 
 
-def from_behind(block, axis, distance):
-    devices = range(lax.axis_size(axis))
-    route = [((i - distance) % len(devices), i) for i in devices]
-    return lax.ppermute(block, axis, route)
-
-
 def rounded(value):
     return value.astype(jnp.bfloat16).astype(jnp.float32)
 
 
-def half(vec_ref, direction, spin, colour, sign):
+def face_table():
+    table = np.zeros((4, 2, 2, 256, 2, 64), np.float32)
+    place = np.arange(64)
+    for mu, stride in enumerate(site_strides):
+        for layer in range(2):
+            site = place // stride * 4 * stride + place % stride + 3 * layer * stride
+            for spin in range(2):
+                table[mu, layer, spin, site, spin, place] = 1.0
+    return table.reshape(4, 2, 512, LANES).astype(jnp.bfloat16)
+
+
+def halved(field, direction, spin, sign):
     pair = []
     for part in range(2):
         from_part, from_spin, factor = lower_table[direction][spin][part]
-        upper = vec_ref[0, part * 12 + spin * 3 + colour].astype(jnp.float32)
-        lower = vec_ref[0, from_part * 12 + from_spin * 3 + colour].astype(jnp.float32)
-        pair.append(rounded(upper + (sign * factor) * lower))
+        lower = field[from_part][from_spin]
+        upper = field[part][spin]
+        pair.append(upper + lower if sign * factor > 0 else upper - lower)
     return pair
 
 
-def link(link_ref, direction, part, row, col):
-    at = direction * 18 + part * 9 + row * 3 + col
-    return link_ref[0, at : at + 1, :]
-
-
-def halves_kernel(vec_ref, link_ref, minus_ref, back_ref):
-    for mu in range(4):
-        for spin in range(2):
-            plus = []
-            for col in range(3):
-                minus = half(vec_ref, mu, spin, col, -1)
-                plus.append(half(vec_ref, mu, spin, col, 1))
-                for part in range(2):
-                    minus_ref[mu, 0, part * 6 + spin * 3 + col] = minus[part].astype(jnp.bfloat16)
-            for col in range(3):
-                out_re, out_im = 0.0, 0.0
-                for row in range(3):
-                    u_re = link(link_ref, mu, 0, row, col)
-                    u_im = link(link_ref, mu, 1, row, col)
-                    p_re, p_im = plus[row]
-                    out_re = out_re + u_re * p_re + u_im * p_im
-                    out_im = out_im + u_re * p_im - u_im * p_re
-                back_ref[mu, 0, spin * 3 + col] = out_re.astype(jnp.bfloat16)
-                back_ref[mu, 0, 6 + spin * 3 + col] = out_im.astype(jnp.bfloat16)
-
-
-def contract(left, right):
-    return lax.dot_general(
-        jnp.concatenate(left, axis=1),
-        jnp.concatenate(right, axis=1),
-        (((1,), (1,)), ((), ())),
-        preferred_element_type=jnp.float32,
-    )
+def link(link_ref, at, direction, part, row, col):
+    index = direction * 18 + part * 9 + row * 3 + col
+    return link_ref[at, index : index + 1, :]
 
 
 def stacked(pieces):
     return jnp.concatenate(pieces, axis=0).astype(jnp.bfloat16)
 
 
+def across(left, right):
+    return lax.dot_general(
+        left, right, (((1,), (1,)), ((), ())), preferred_element_type=jnp.float32
+    )
+
+
+def packed(operand, table):
+    rows = jnp.concatenate([operand[:, at * 512 : (at + 1) * 512] for at in range(3)], axis=0)
+    out = jnp.dot(rows, table, preferred_element_type=jnp.float32)
+    return [out[at * 2 * NV : (at + 1) * 2 * NV] for at in range(3)]
+
+
+def store_face(ref, index, pieces):
+    for at, piece in enumerate(pieces):
+        ref[index + (slice(None), slice(at * LANES, (at + 1) * LANES))] = piece.astype(jnp.bfloat16)
+
+
+def faces_kernel(vec_ref, link_ref, table_ref, face_ref):
+    field = [
+        [
+            [vec_ref[0, part * 12 + spin * 3 + col].astype(jnp.float32) for spin in range(4)]
+            for part in range(2)
+        ]
+        for col in range(3)
+    ]
+    for mu in range(3):
+        sides = []
+        for sign in (-1, 1):
+            pieces = []
+            for col in range(3):
+                for spin in range(2):
+                    pieces.append(stacked(halved(field[col], mu, spin, sign)))
+            sides.append(jnp.concatenate(pieces, axis=1))
+        store_face(face_ref, (2 * mu, 0), packed(sides[0], table_ref[mu, 0]))
+        plus = packed(sides[1], table_ref[mu, 1])
+        rows = link_ref[0, mu * 18 : (mu + 1) * 18, :].astype(jnp.bfloat16)
+        links = jnp.dot(
+            rows, table_ref[mu, 1, :256], preferred_element_type=jnp.float32
+        ) + jnp.dot(rows, table_ref[mu, 1, 256:], preferred_element_type=jnp.float32)
+        back = []
+        for col in range(3):
+            out_re, out_im = 0.0, 0.0
+            for row in range(3):
+                at = row * 3 + col
+                u_re, u_im = links[at : at + 1], links[9 + at : 10 + at]
+                p_re, p_im = plus[row][:NV], plus[row][NV:]
+                out_re = out_re + u_re * p_re + u_im * p_im
+                out_im = out_im + u_re * p_im - u_im * p_re
+            back.append(jnp.concatenate([out_re, out_im], axis=0))
+        store_face(face_ref, (2 * mu + 1, 0), back)
+
+
 def merged(product):
     lane = lax.broadcasted_iota(jnp.int32, (NV, LANES), 1)
-    wide = jnp.concatenate([product, jnp.zeros((2 * NV, LANES - 4 * NV), jnp.float32)], axis=1)
+    wide = jnp.concatenate([product, jnp.zeros((2 * NV, LANES - 2 * NV), jnp.float32)], axis=1)
     low = wide[NV:]
-    crossed = jnp.where(
-        lane // NV % 2 == 0, pltpu.roll(low, LANES - NV, 1), -pltpu.roll(low, NV, 1)
-    )
+    crossed = jnp.where(lane < NV, pltpu.roll(low, LANES - NV, 1), -pltpu.roll(low, NV, 1))
     return wide[:NV] + crossed
 
 
-def restrict_kernel(vec_ref, link_ref, site_ref, rhs_ref, minus_ref, back_ref, *rest):
-    near_minus, near_back = rest[0:4], rest[4:8]
-    msg_ref, block_ref, flat_ref = rest[8:]
-    step = pl.program_id(0)
+def fine_kernel(
+    face_ref, vec_ref, link_ref, site_ref, rhs_ref, table_ref, msg_ref,
+    near_ref, field_ref, left_ref, time_ref, own_ref, block_ref, flat_ref, send_sem, recv_sem,
+):
     sites = vec_ref.shape[-1]
+    axes = ("gx", "gy", "gz")
+    here = {name: lax.axis_index(name) for name in axes}
+
+    def beside(mu, step):
+        size = lax.axis_size(axes[mu])
+        place = dict(here)
+        place[axes[mu]] = (here[axes[mu]] + step + size) % size
+        return (place["gz"], place["gy"], place["gx"])
+
+    barrier = pltpu.get_barrier_semaphore()
+    for mu in range(3):
+        for step in (-1, 1):
+            pl.semaphore_signal(
+                barrier, inc=1, device_id=beside(mu, step), device_id_type=MESH
+            )
+    pl.semaphore_wait(barrier, 6)
+    copies = []
+    for mu in (0, 2, 1):
+        for side, step in enumerate((-1, 1)):
+            at = 2 * mu + side
+            copies.append(
+                pltpu.make_async_remote_copy(
+                    src_ref=face_ref.at[at],
+                    dst_ref=near_ref.at[at],
+                    send_sem=send_sem.at[at],
+                    recv_sem=recv_sem.at[at],
+                    device_id=beside(mu, step),
+                    device_id_type=MESH,
+                )
+            )
+    for item in copies:
+        item.start()
+
+    position = lax.broadcasted_iota(jnp.int32, (NV, sites), 1)
     lane8 = lax.broadcasted_iota(jnp.int32, (8, LANES), 1)
     block_ref[NV:] = jnp.zeros((block_ref.shape[0] - NV, LANES), jnp.float32)
 
-    def emit(k, block):
-        block_ref[:NV] = rounded(block)
-        pieces = [jnp.zeros((8, LANES), jnp.float32)] * 2
-        for at in range(GROUP):
-            rows = block_ref[pl.ds(at, 8, stride=GROUP), :]
+    @pl.loop(0, AT)
+    def _(a):
+        field_ref[...] = vec_ref[a].astype(jnp.float32)
+
+        def value(part, spin, col):
+            return field_ref[part * 12 + spin * 3 + col]
+
+        left, right = [], []
+        for chirality in range(2):
+            for i in range(6):
+                out_re, out_im = 0.0, 0.0
+                for j in range(6):
+                    at = chirality * 72 + i * 6 + j
+                    m_re = site_ref[a, at : at + 1, :]
+                    m_im = site_ref[a, at + 36 : at + 37, :]
+                    v_re = field_ref[chirality * 6 + j]
+                    v_im = field_ref[12 + chirality * 6 + j]
+                    out_re = out_re + m_re * v_re - m_im * v_im
+                    out_im = out_im + m_re * v_im + m_im * v_re
+                right.append(stacked([out_re, out_im]))
+                at = chirality * 6 + i
+                left.append(stacked([field_ref[at], field_ref[12 + at]]))
+        own = merged(across(jnp.concatenate(left, axis=1), jnp.concatenate(right, axis=1)))
+        for mu in range(4):
+            stride = site_strides[mu]
+            last = position // stride % 4 == 3
+            turned_minus, turned_plus, ahead_minus, ahead_plus, plain_minus, plain_plus = (
+                [] for _ in range(6)
+            )
+            for col in range(3):
+                turned = [[], []]
+                for spin in range(4):
+                    out_re, out_im = 0.0, 0.0
+                    for row in range(3):
+                        u_re = link(link_ref, a, mu, 0, row, col)
+                        u_im = link(link_ref, a, mu, 1, row, col)
+                        v_re, v_im = value(0, spin, row), value(1, spin, row)
+                        out_re = out_re + u_re * v_re + u_im * v_im
+                        out_im = out_im + u_re * v_im - u_im * v_re
+                    turned[0].append(out_re)
+                    turned[1].append(out_im)
+                plain = [[value(part, spin, col) for spin in range(4)] for part in range(2)]
+                ahead = [
+                    [jnp.where(last, 0.0, pltpu.roll(item, sites - stride, 1)) for item in items]
+                    for items in plain
+                ]
+                for spin in range(2):
+                    turned_minus.append(stacked(halved(turned, mu, spin, -1)))
+                    turned_plus.append(stacked(halved(turned, mu, spin, 1)))
+                    ahead_minus.append(stacked(halved(ahead, mu, spin, -1)))
+                    ahead_plus.append(stacked(halved(ahead, mu, spin, 1)))
+                    plain_plus.append(stacked(halved(plain, mu, spin, 1)))
+                    if mu == 3:
+                        plain_minus.append(stacked(halved(plain, mu, spin, -1)))
+            turned_minus = jnp.concatenate(turned_minus, axis=1)
+            turned_plus = jnp.concatenate(turned_plus, axis=1)
+            both = across(
+                jnp.concatenate([turned_minus] + ahead_plus, axis=1),
+                jnp.concatenate(ahead_minus + [turned_plus], axis=1),
+            )
+            own = own - 0.5 * merged(both)
+            store_face(left_ref, (a, 2 * mu), packed(turned_minus, table_ref[mu, 1]))
+            store_face(
+                left_ref,
+                (a, 2 * mu + 1),
+                packed(jnp.concatenate(plain_plus, axis=1), table_ref[mu, 0]),
+            )
+            if mu == 3:
+                store_face(
+                    time_ref, (0, a), packed(jnp.concatenate(plain_minus, axis=1), table_ref[mu, 0])
+                )
+                store_face(time_ref, (1, a), packed(turned_plus, table_ref[mu, 1]))
+        own_ref[a] = own * coarse_scale
+
+    for item in copies:
+        item.wait_recv()
+
+    @pl.loop(0, AT)
+    def _(a):
+        for k in range(9):
+            if k == 0:
+                block = own_ref[a]
+            else:
+                mu, side = (k - 1) // 2, (k - 1) % 2
+                if mu < 3:
+                    near = near_ref[k - 1, a]
+                else:
+                    near = time_ref[side, (a + 1 + 2 * side) % AT]
+                block = merged(across(left_ref[a, k - 1], near)) * (-0.5 * coarse_scale)
+            block_ref[:NV] = rounded(block)
+            pieces = [jnp.zeros((8, LANES), jnp.float32)] * 2
+            for at in range(GROUP):
+                rows = block_ref[pl.ds(at, 8, stride=GROUP), :]
+                for part in range(2):
+                    shift = (at - part) * NV % LANES
+                    moved = rows if shift == 0 else pltpu.roll(rows, shift, 1)
+                    pieces[part] = jnp.where(lane8 // NV == at, moved, pieces[part])
             for part in range(2):
-                shift = (at - part) * NV % LANES
-                moved = rows if shift == 0 else pltpu.roll(rows, shift, 1)
-                pieces[part] = jnp.where(lane8 // NV == at, moved, pieces[part])
-        for part in range(2):
-            flat_ref[k, pl.ds(pl.multiple_of(step * 16 + part * 8, 8), 8), :] = pieces[part]
-
-    left, right = [], []
-    for chirality in range(2):
-        for i in range(6):
-            out_re, out_im = 0.0, 0.0
-            for j in range(6):
-                at = chirality * 72 + i * 6 + j
-                m_re = site_ref[0, at : at + 1, :]
-                m_im = site_ref[0, at + 36 : at + 37, :]
-                v_re = vec_ref[0, chirality * 6 + j].astype(jnp.float32)
-                v_im = vec_ref[0, 12 + chirality * 6 + j].astype(jnp.float32)
-                out_re = out_re + m_re * v_re - m_im * v_im
-                out_im = out_im + m_re * v_im + m_im * v_re
-            right.append(stacked([out_re, out_im, out_re, out_im]))
-            at = chirality * 6 + i
-            left.append(
-                stacked([vec_ref[0, at].astype(jnp.float32), vec_ref[0, 12 + at].astype(jnp.float32)])
+                flat_ref[k, pl.ds(pl.multiple_of(a * 16 + part * 8, 8), 8), :] = pieces[part]
+
+    for k in range(9):
+        for chunk in range(CHUNKS):
+            at = (k * CHUNKS + chunk) * LANES
+            msg_ref[:, at : at + LANES] = flat_ref[k, pl.ds(chunk, ROWS, stride=8), :].astype(
+                jnp.bfloat16
             )
-    own = merged(contract(left, right))
-    position = lax.broadcasted_iota(jnp.int32, (NV, sites), 1)
-    for mu in range(4):
-        stride = site_strides[mu]
-        coordinate = position // stride % 4
-        last = coordinate == 3
-        first = coordinate == 0
-
-        def split(pair, edge):
-            return stacked(
-                [jnp.where(edge, 0.0, part) for part in pair]
-                + [jnp.where(edge, part, 0.0) for part in pair]
-            )
-
-        def shifted(own, near, edge, own_shift, near_shift):
-            return jnp.where(
-                edge,
-                pltpu.roll(near.astype(jnp.float32), near_shift, 1),
-                pltpu.roll(own.astype(jnp.float32), own_shift, 1),
-            )
-
-        left, right = [], []
-        for spin in range(2):
-            field = []
-            for col in range(3):
-                at = spin * 3 + col
-                field.append(
-                    [
-                        shifted(
-                            minus_ref[mu, 0, part * 6 + at],
-                            near_minus[mu][0, part * 6 + at],
-                            last,
-                            sites - stride,
-                            3 * stride,
-                        )
-                        for part in range(2)
-                    ]
-                )
-            for row in range(3):
-                out_re, out_im = 0.0, 0.0
-                for col in range(3):
-                    u_re = link(link_ref, mu, 0, row, col)
-                    u_im = link(link_ref, mu, 1, row, col)
-                    f_re, f_im = field[col]
-                    out_re = out_re + u_re * f_re - u_im * f_im
-                    out_im = out_im + u_re * f_im + u_im * f_re
-                right.append(split((out_re, out_im), last))
-                at = spin * 3 + row
-                left.append(
-                    stacked([minus_ref[mu, 0, part * 6 + at].astype(jnp.float32) for part in range(2)])
-                )
-        both = merged(contract(left, right))
-        own = own - 0.5 * both
-        emit(2 * mu + 1, pltpu.roll(both, LANES - 2 * NV, 1) * (-0.5 * coarse_scale))
-        left, right = [], []
-        for spin in range(2):
-            for col in range(3):
-                at = spin * 3 + col
-                pair = [
-                    shifted(
-                        back_ref[mu, 0, part * 6 + at],
-                        near_back[mu][0, part * 6 + at],
-                        first,
-                        stride,
-                        sites - 3 * stride,
-                    )
-                    for part in range(2)
-                ]
-                right.append(split(pair, first))
-                left.append(stacked(half(vec_ref, mu, spin, col, 1)))
-        both = merged(contract(left, right))
-        own = own - 0.5 * both
-        emit(2 * mu + 2, pltpu.roll(both, LANES - 2 * NV, 1) * (-0.5 * coarse_scale))
-    emit(0, own * coarse_scale)
-
-    @pl.when(step == AT - 1)
-    def _():
-        for k in range(9):
-            for chunk in range(CHUNKS):
-                at = (k * CHUNKS + chunk) * LANES
-                msg_ref[:, at : at + LANES] = flat_ref[
-                    k, pl.ds(chunk, ROWS, stride=8), :
-                ].astype(jnp.bfloat16)
-        msg_ref[:, TILES * LANES :] = rhs_ref[...]
+    msg_ref[:, TILES * LANES :] = rhs_ref[...]
+    for item in copies:
+        item.wait_send()
 
 
 def fine_message(vectors, links, site_term, rhs):
@@ -243,39 +285,41 @@
     tiled = jnp.concatenate(
         [rhs.reshape(ROWS, NV)] * GROUP + [jnp.zeros((ROWS, LANES - GROUP * NV), rhs.dtype)], axis=1
     )
-    vec_spec = pl.BlockSpec((1, 24, NV, sites), lambda a: (a, 0, 0, 0))
-    link_spec = pl.BlockSpec((1, 72, sites), lambda a: (a, 0, 0))
-    site_spec = pl.BlockSpec((1, 144, sites), lambda a: (a, 0, 0))
-    rhs_spec = pl.BlockSpec((ROWS, LANES), lambda a: (0, 0))
-    half_spec = pl.BlockSpec((4, 1, 12, NV, sites), lambda a: (0, a, 0, 0, 0))
-    near_spec = pl.BlockSpec((1, 12, NV, sites), lambda a: (a, 0, 0, 0))
-    half_shape = jax.ShapeDtypeStruct((4, AT, 12, NV, sites), jnp.bfloat16)
-    params = pltpu.CompilerParams(vmem_limit_bytes=48 << 20)
-    minus, back = pl.pallas_call(
-        halves_kernel,
+    table = face_table()
+    face = (2 * NV, 3 * LANES)
+    faces = pl.pallas_call(
+        faces_kernel,
         grid=(AT,),
-        in_specs=[vec_spec, link_spec],
-        out_specs=[half_spec, half_spec],
-        out_shape=(half_shape, half_shape),
-        compiler_params=params,
-    )(vec, link_f)
-    axes = ("gx", "gy", "gz")
-    near_minus = [from_behind(minus[mu], axes[mu], -1) for mu in range(3)]
-    near_back = [from_behind(back[mu], axes[mu], 1) for mu in range(3)]
-    near_minus.append(jnp.roll(minus[3], -1, axis=0))
-    near_back.append(jnp.roll(back[3], 1, axis=0))
+        in_specs=[
+            pl.BlockSpec((1, 24, NV, sites), lambda a: (a, 0, 0, 0)),
+            pl.BlockSpec((1, 72, sites), lambda a: (a, 0, 0)),
+            pl.BlockSpec(table.shape, lambda a: (0, 0, 0, 0)),
+        ],
+        out_specs=pl.BlockSpec((6, 1) + face, lambda a: (0, a, 0, 0)),
+        out_shape=jax.ShapeDtypeStruct((6, AT) + face, jnp.bfloat16),
+        compiler_params=pltpu.CompilerParams(vmem_limit_bytes=32 << 20),
+    )(vec, link_f, table)
+    vmem = pl.BlockSpec(memory_space=pltpu.VMEM)
     return pl.pallas_call(
-        restrict_kernel,
-        grid=(AT,),
-        in_specs=[vec_spec, link_spec, site_spec, rhs_spec, half_spec, half_spec] + [near_spec] * 8,
-        out_specs=pl.BlockSpec((ROWS, WIDE), lambda a: (0, 0)),
+        fine_kernel,
+        in_specs=[vmem] * 6,
+        out_specs=vmem,
         out_shape=jax.ShapeDtypeStruct((ROWS, WIDE), jnp.bfloat16),
         scratch_shapes=[
+            pltpu.VMEM((6, AT) + face, jnp.bfloat16),
+            pltpu.VMEM((24, NV, sites), jnp.float32),
+            pltpu.VMEM((AT, 8) + face, jnp.bfloat16),
+            pltpu.VMEM((2, AT) + face, jnp.bfloat16),
+            pltpu.VMEM((AT, NV, LANES), jnp.float32),
             pltpu.VMEM((8 * GROUP, LANES), jnp.float32),
             pltpu.VMEM((9, 8 * ROWS, LANES), jnp.float32),
+            pltpu.SemaphoreType.DMA((6,)),
+            pltpu.SemaphoreType.DMA((6,)),
         ],
-        compiler_params=params,
-    )(vec, link_f, site_f, tiled, minus, back, *near_minus, *near_back)
+        compiler_params=pltpu.CompilerParams(
+            collective_id=2, has_side_effects=True, vmem_limit_bytes=32 << 20
+        ),
+    )(faces, vec, link_f, site_f, tiled, table)
 
 
 def complex_mul(first, second):

time: 94.6 us -> 66.7 us (0.71)
  waiting for transfers between devices: 20.2 us -> 0 us
  starting transfers between devices: 9.25 us -> 0 us
  Pallas kernels: 52.7 us -> 56.4 us
  local copies, waits for them, and re-layouts: 10.2 us -> 8.1 us
    ppermute x6 -> x0, waiting for transfers between devices: 20.2 us -> none  [from_behind(): return lax.ppermute(block, axis, route)]
    ppermute x6 -> x0, starting transfers between devices: 9.25 us -> none  [from_behind(): return lax.ppermute(block, axis, route)]
    pallas_call x2, Pallas kernels: 14.3 us -> 18.8 us  [the longest x1 16.7 us: fine_message(): pl.pallas_call(fine_kernel, in_specs=[vmem] * 6, out_specs=vmem, out_shap...]
    squeeze x2 -> x0, local copies, waits for them, and re-layouts: 2.56 us -> none  [the longest x1 1.33 us: fine_message(): near_minus = [from_behind(minus[mu], axes[mu], -1) for mu in range(3)]]
    slice x2 -> x0, local copies, waits for them, and re-layouts: 2 us -> none  [fine_message(): near_back.append(jnp.roll(back[3], 1, axis=0))]
    unnamed x15 -> x9, local copies, waits for them, and re-layouts: 3.06 us -> 5.01 us
    transpose x1, local copies, waits for them, and re-layouts: 1.54 us -> 0.24 us  [fine_message(): vec = jnp.transpose(vectors, (0, 2, 3, 4, 1, 5)).reshape(AT, 24, NV, sites)]
    pallas_call x1, Pallas kernels: 22.6 us -> 21.6 us  [gather_messages(): pl.pallas_call(gather_kernel, out_shape=jax.ShapeDtypeStruct((devices, RO...]
  transfers between devices with their start and end apart: 6 -> 0, of which waited for: 3 -> 0; matrix products, arithmetic and copies ran while one was open for 6% -> 0% of each run, Pallas kernels for 0% -> 0%
where the time goes in v2:
time: 66.7 us; the launch traced here: 66.2 us
  Pallas kernels  56.4 us (85%)
  local copies, waits for them, and re-layouts  8.1 us (12%)
  other arithmetic  0.93 us (1%)
  between operations  0.74 us (1%)
    pallas_call x1, Pallas kernels, gather_messages(): pl.pallas_call(gather_kernel, out_shape=jax.ShapeDtypeStruct((devices, RO...  21.6 us
    pallas_call x1, Pallas kernels, fine_message(): pl.pallas_call(fine_kernel, in_specs=[vmem] * 6, out_specs=vmem, out_shap...  16.7 us
    pallas_call x1, Pallas kernels, coarse_solve(): pl.pallas_call(lambda *refs: gmres_kernel(sizes, *refs), out_shape=(jax.S...  16 us
    unnamed x9, local copies, waits for them, and re-layouts  5.01 us
    pallas_call x1, Pallas kernels, fine_message(): pl.pallas_call(faces_kernel, grid=(AT,), in_specs=[pl.BlockSpec((1, 24, N...  2.06 us

profile of v2, /device:TPU:0, one launch (start us, length us, event | category | flops | bytes accessed | tf_op | source)
XLA Modules:
  0.0 66.2 jit_solution(15174749929131532705)
XLA Ops:
  0.6 0.0 copy-start.3
  0.7 1.0 %concatenate.3.rhs_ref = bf16[8,128]{1,0:T(8,128)(2,1)S(1)} concatenate(bf16[8,24]{1,0:T(8,128)(2,1)} %bitcast.14, bf16[8,24]{1,0:T(8,128)(2,1)} %bitcast.15, bf16[8,24]{1,0:T(8,128)(2,1)} %bitcast.16, bf16[8,24]{1,0:T(8,128)(2,1)} %bitcast.17, bf16[8,24]{1,0:T(8,128)(2,1)} %bitcast.18, bf16[8,8]{1,0:T(8,128)(2,1)S(1)} %broadcast_in_dim.19), dimensions={1} | concatenate | bytes 4096 | tf_op jit(solution)/shard_map/concatenate | solution.py:285
  1.6 0.9 %select_reduce_fusion = s32[4,2,4]{2,1,0:T(2,128)S(1)} fusion(s32[4,2,4,4]{3,2,1,0:T(4,128)} %param.10, s32[]{:T(128)S(6)} %add.3), kind=kLoop, calls=%fused_computation | loop fusion | flops 352 | bytes 644 | tf_op jit(solution)/shard_map/reduce_max | solution.py:747
  2.5 0.6 reduce_max.12.refs_0_
  3.2 1.0 %copy.14 = f32[1,1,1,4,4,2,3,3,256]{8,3,7,6,5,4,2,1,0:T(4,128)S(1)} copy(bf16[1,1,1,4,4,2,3,3,256]{8,5,7,6,4,3,2,1,0:T(2,128)(2,1)} %param.8) | data formatting | bytes 442368 | tf_op jit(solution)/shard_map/convert_element_type | solution.py:283
  4.1 0.1 copy.15.link_ref
  4.2 0.0 copy-done.3
  4.2 0.0 copy-start.2
  4.2 0.2 copy.16
  4.4 0.1 copy.18.site_ref
  4.5 1.0 %copy-done.2 = bf16[1,1,1,4,24,2,4,3,256]{8,6,7,5,4,3,2,1,0:T(4,128)(2,1)S(1)} copy-done((bf16[1,1,1,4,24,2,4,3,256]{8,6,7,5,4,3,2,1,0:T(4,128)(2,1)S(1)}, bf16[1,1,1,4,24,2,4,3,256]{8,6,7,5,4,3,2,1,0:T(4,128)(2,1)}, u32[]{:S(2)}) %copy-start.2) | copy-done | bytes 1179672
  5.5 0.0 copy-start.1
  5.5 0.2 copy.13
  5.7 1.0 %copy-done.1 = bf16[4,2,512,128]{3,2,1,0:T(8,128)(2,1)S(1)} copy-done((bf16[4,2,512,128]{3,2,1,0:T(8,128)(2,1)S(1)}, bf16[4,2,512,128]{3,2,1,0:T(8,128)(2,1)}, u32[]{:S(2)}) %copy-start.1) | copy-done | bytes 1048600
  6.7 2.1 %shard_map.86.face_ref = bf16[6,4,48,384]{3,2,1,0:T(8,128)(2,1)S(1)} custom-call(bf16[4,24,24,256]{3,2,1,0:T(8,128)(2,1)S(1)} %bitcast.9, f32[4,72,256]{2,1,0:T(8,128)S(1)} %copy.15.link_ref, bf16[4,2,512,128]{3,2,1,0:T(8,128)(2,1)S(1)} %copy-done.1), custom_call_target="tpu_custom_call" | custom-call | tf_op jit(solution)/shard_map/pallas_call | solution.py:290
  8.8 16.7 %shard_map.87.msg_ref = bf16[8,5888]{1,0:T(8,128)(2,1)S(1)} custom-call(bf16[6,4,48,384]{3,2,1,0:T(8,128)(2,1)S(1)} %shard_map.86.face_ref, bf16[4,24,24,256]{3,2,1,0:T(8,128)(2,1)S(1)} %bitcast.10, f32[4,72,256]{2,1,0:T(8,128)S(1)} %copy.15.link_ref, f32[4,144,256]{2,1,0:T(8,128)S(1)} %copy.18.site_ref, bf16[8,128]{1,0:T(8,128)(2,1)S(1)} %concatenate.3.rhs_ref, ...), custom_call_target="tpu_custom_call" | custom-call | tf_op jit(solution)/shard_map/pallas_call | solution.py:303
  25.5 21.6 %shard_map.88.refs_1_ = bf16[32,8,5888]{2,1,0:T(8,128)(2,1)S(1)} custom-call(bf16[8,5888]{1,0:T(8,128)(2,1)S(1)} %shard_map.87.msg_ref), custom_call_target="tpu_custom_call" | custom-call | tf_op jit(solution)/shard_map/pallas_call | solution.py:562
  47.1 0.0 copy-start
  47.1 1.6 %copy-done = bf16[32,8,5888]{2,1,0:T(8,128)(2,1)} copy-done((bf16[32,8,5888]{2,1,0:T(8,128)(2,1)}, bf16[32,8,5888]{2,1,0:T(8,128)(2,1)S(1)}, u32[]{:S(2)}) %copy-start) | copy-done | bytes 3014680
  48.7 16.0 %shard_map.89 = (bf16[32,9,2,576]{3,2,1,0:T(2,128)(2,1)}, f32[32,2,24]{2,1,0:T(2,128)}) custom-call(s32[32]{0:T(128)} %reduce_max.12.refs_0_, bf16[32,8,5888]{2,1,0:T(8,128)(2,1)} %copy-done, bf16[640,128]{1,0:T(8,128)(2,1)} %constant.20.clone.refs_2_), custom_call_target="tpu_custom_call" | custom-call | tf_op jit(solution)/shard_map/pallas_call | solution.py:749
  64.8 1.4 %copy.19 = f32[1,32,2,24]{1,3,2,0:T(8,128)} copy(f32[1,32,2,24]{3,2,1,0:T(2,128)} %bitcast.19) | data formatting | bytes 12288
  (1 shorter events, 0.0 us)
Async XLA Ops:
  0.6 3.6 %copy-start.3 = (bf16[1,1,1,4,2,2,6,6,256]{8,5,7,6,4,3,2,1,0:T(2,128)(2,1)S(1)}, bf16[1,1,1,4,2,2,6,6,256]{8,5,7,6,4,3,2,1,0:T(2,128)(2,1)}, u32[]{:S(2)}) copy-start(bf16[1,1,1,4,2,2,6,6,256]{8,5,7,6,4,3,2,1,0:T(2,128)(2,1)} %param.9) | copy-start | bytes 884740
  4.2 1.3 %copy-start.2 = (bf16[1,1,1,4,24,2,4,3,256]{8,6,7,5,4,3,2,1,0:T(4,128)(2,1)S(1)}, bf16[1,1,1,4,24,2,4,3,256]{8,6,7,5,4,3,2,1,0:T(4,128)(2,1)}, u32[]{:S(2)}) copy-start(bf16[1,1,1,4,24,2,4,3,256]{8,6,7,5,4,3,2,1,0:T(4,128)(2,1)} %param.7) | copy-start | bytes 3538948
  5.5 1.2 %copy-start.1 = (bf16[4,2,512,128]{3,2,1,0:T(8,128)(2,1)S(1)}, bf16[4,2,512,128]{3,2,1,0:T(8,128)(2,1)}, u32[]{:S(2)}) copy-start(bf16[4,2,512,128]{3,2,1,0:T(8,128)(2,1)} %constant.19.clone.table_ref) | copy-start | bytes 3145732
  47.1 1.6 %copy-start = (bf16[32,8,5888]{2,1,0:T(8,128)(2,1)}, bf16[32,8,5888]{2,1,0:T(8,128)(2,1)S(1)}, u32[]{:S(2)}) copy-start(bf16[32,8,5888]{2,1,0:T(8,128)(2,1)S(1)} %shard_map.88.refs_1_) | copy-start | bytes 9043972

commit v3 on v2

--- a/solution.py
+++ b/solution.py
@@ -34,15 +34,12 @@
     return value.astype(jnp.bfloat16).astype(jnp.float32)
 
 
-def face_table():
-    table = np.zeros((4, 2, 2, 256, 2, 64), np.float32)
-    place = np.arange(64)
-    for mu, stride in enumerate(site_strides):
-        for layer in range(2):
-            site = place // stride * 4 * stride + place % stride + 3 * layer * stride
-            for spin in range(2):
-                table[mu, layer, spin, site, spin, place] = 1.0
-    return table.reshape(4, 2, 512, LANES).astype(jnp.bfloat16)
+def face_table(stride, layer):
+    row = lax.broadcasted_iota(jnp.int32, (512, LANES), 0)
+    lane = lax.broadcasted_iota(jnp.int32, (512, LANES), 1)
+    place = lane % 64
+    site = place // stride * 4 * stride + place % stride + 3 * layer * stride
+    return jnp.where(row == site + lane // 64 * 256, 1.0, 0.0).astype(jnp.bfloat16)
 
 
 def halved(field, direction, spin, sign):
@@ -55,9 +52,9 @@
     return pair
 
 
-def link(link_ref, at, direction, part, row, col):
-    index = direction * 18 + part * 9 + row * 3 + col
-    return link_ref[at, index : index + 1, :]
+def link(link_ref, direction, part, row, col):
+    index = (direction * 9 + row * 3 + col) * 2 + part
+    return link_ref[index : index + 1, :]
 
 
 def stacked(pieces):
@@ -81,7 +78,13 @@
         ref[index + (slice(None), slice(at * LANES, (at + 1) * LANES))] = piece.astype(jnp.bfloat16)
 
 
-def faces_kernel(vec_ref, link_ref, table_ref, face_ref):
+def faces_kernel(vec_ref, link_ref, face_ref, table_ref, row_ref):
+    @pl.when(pl.program_id(0) == 0)
+    def _():
+        for mu in range(3):
+            for layer in range(2):
+                table_ref[mu, layer] = face_table(site_strides[mu], layer)
+
     field = [
         [
             [vec_ref[0, part * 12 + spin * 3 + col].astype(jnp.float32) for spin in range(4)]
@@ -99,7 +102,11 @@
             sides.append(jnp.concatenate(pieces, axis=1))
         store_face(face_ref, (2 * mu, 0), packed(sides[0], table_ref[mu, 0]))
         plus = packed(sides[1], table_ref[mu, 1])
-        rows = link_ref[0, mu * 18 : (mu + 1) * 18, :].astype(jnp.bfloat16)
+        for row in range(3):
+            for col in range(3):
+                at = (row * 3 + col) * 2
+                row_ref[mu, at : at + 2] = link_ref[0, mu, row, col].astype(jnp.float32)
+        rows = row_ref[mu].astype(jnp.bfloat16)
         links = jnp.dot(
             rows, table_ref[mu, 1, :256], preferred_element_type=jnp.float32
         ) + jnp.dot(rows, table_ref[mu, 1, 256:], preferred_element_type=jnp.float32)
@@ -107,8 +114,8 @@
         for col in range(3):
             out_re, out_im = 0.0, 0.0
             for row in range(3):
-                at = row * 3 + col
-                u_re, u_im = links[at : at + 1], links[9 + at : 10 + at]
+                at = (row * 3 + col) * 2
+                u_re, u_im = links[at : at + 1], links[at + 1 : at + 2]
                 p_re, p_im = plus[row][:NV], plus[row][NV:]
                 out_re = out_re + u_re * p_re + u_im * p_im
                 out_im = out_im + u_re * p_im - u_im * p_re
@@ -125,8 +132,9 @@
 
 
 def fine_kernel(
-    face_ref, vec_ref, link_ref, site_ref, rhs_ref, table_ref, msg_ref,
-    near_ref, field_ref, left_ref, time_ref, own_ref, block_ref, flat_ref, send_sem, recv_sem,
+    face_ref, vec_ref, raw_link_ref, raw_site_ref, rhs_ref, msg_ref,
+    near_ref, field_ref, left_ref, time_ref, own_ref, block_ref, flat_ref,
+    table_ref, link_ref, site_ref, side_ref, send_sem, recv_sem,
 ):
     sites = vec_ref.shape[-1]
     axes = ("gx", "gy", "gz")
@@ -165,10 +173,19 @@
     position = lax.broadcasted_iota(jnp.int32, (NV, sites), 1)
     lane8 = lax.broadcasted_iota(jnp.int32, (8, LANES), 1)
     block_ref[NV:] = jnp.zeros((block_ref.shape[0] - NV, LANES), jnp.float32)
+    for mu in range(4):
+        for layer in range(2):
+            table_ref[mu, layer] = face_table(site_strides[mu], layer)
 
     @pl.loop(0, AT)
     def _(a):
         field_ref[...] = vec_ref[a].astype(jnp.float32)
+        for at in range(36):
+            mu, row, col = at // 9, at // 3 % 3, at % 3
+            link_ref[2 * at : 2 * at + 2] = raw_link_ref[a, mu, row, col].astype(jnp.float32)
+        for at in range(72):
+            chirality, row, col = at // 36, at // 6 % 6, at % 6
+            site_ref[2 * at : 2 * at + 2] = raw_site_ref[a, chirality, row, col].astype(jnp.float32)
 
         def value(part, spin, col):
             return field_ref[part * 12 + spin * 3 + col]
@@ -178,9 +195,9 @@
             for i in range(6):
                 out_re, out_im = 0.0, 0.0
                 for j in range(6):
-                    at = chirality * 72 + i * 6 + j
-                    m_re = site_ref[a, at : at + 1, :]
-                    m_im = site_ref[a, at + 36 : at + 37, :]
+                    at = (chirality * 36 + i * 6 + j) * 2
+                    m_re = site_ref[at : at + 1, :]
+                    m_im = site_ref[at + 1 : at + 2, :]
                     v_re = field_ref[chirality * 6 + j]
                     v_im = field_ref[12 + chirality * 6 + j]
                     out_re = out_re + m_re * v_re - m_im * v_im
@@ -200,8 +217,8 @@
                 for spin in range(4):
                     out_re, out_im = 0.0, 0.0
                     for row in range(3):
-                        u_re = link(link_ref, a, mu, 0, row, col)
-                        u_im = link(link_ref, a, mu, 1, row, col)
+                        u_re = link(link_ref, mu, 0, row, col)
+                        u_im = link(link_ref, mu, 1, row, col)
                         v_re, v_im = value(0, spin, row), value(1, spin, row)
                         out_re = out_re + u_re * v_re + u_im * v_im
                         out_im = out_im + u_re * v_im - u_im * v_re
@@ -272,7 +289,12 @@
             msg_ref[:, at : at + LANES] = flat_ref[k, pl.ds(chunk, ROWS, stride=8), :].astype(
                 jnp.bfloat16
             )
-    msg_ref[:, TILES * LANES :] = rhs_ref[...]
+    for a in range(AT):
+        rhs = rhs_ref[a].astype(jnp.float32)
+        side_ref[2 * a : 2 * a + 2] = jnp.concatenate(
+            [rhs] * GROUP + [jnp.zeros((2, LANES - GROUP * NV), jnp.float32)], axis=1
+        )
+    msg_ref[:, TILES * LANES :] = side_ref[...].astype(jnp.bfloat16)
     for item in copies:
         item.wait_send()
 
@@ -280,29 +302,28 @@
 def fine_message(vectors, links, site_term, rhs):
     sites = vectors.shape[-1]
     vec = jnp.transpose(vectors, (0, 2, 3, 4, 1, 5)).reshape(AT, 24, NV, sites)
-    link_f = links.astype(jnp.float32).reshape(AT, 72, sites)
-    site_f = site_term.astype(jnp.float32).reshape(AT, 144, sites)
-    tiled = jnp.concatenate(
-        [rhs.reshape(ROWS, NV)] * GROUP + [jnp.zeros((ROWS, LANES - GROUP * NV), rhs.dtype)], axis=1
-    )
-    table = face_table()
+    link_rows = jnp.transpose(links, (0, 1, 3, 4, 2, 5))
+    site_rows = jnp.transpose(site_term, (0, 1, 3, 4, 2, 5))
     face = (2 * NV, 3 * LANES)
     faces = pl.pallas_call(
         faces_kernel,
         grid=(AT,),
         in_specs=[
             pl.BlockSpec((1, 24, NV, sites), lambda a: (a, 0, 0, 0)),
-            pl.BlockSpec((1, 72, sites), lambda a: (a, 0, 0)),
-            pl.BlockSpec(table.shape, lambda a: (0, 0, 0, 0)),
+            pl.BlockSpec((1, 4, 3, 3, 2, sites), lambda a: (a, 0, 0, 0, 0, 0)),
         ],
         out_specs=pl.BlockSpec((6, 1) + face, lambda a: (0, a, 0, 0)),
         out_shape=jax.ShapeDtypeStruct((6, AT) + face, jnp.bfloat16),
-        compiler_params=pltpu.CompilerParams(vmem_limit_bytes=32 << 20),
-    )(vec, link_f, table)
+        scratch_shapes=[
+            pltpu.VMEM((3, 2, 512, LANES), jnp.bfloat16),
+            pltpu.VMEM((3, 18, sites), jnp.float32),
+        ],
+        compiler_params=pltpu.CompilerParams(vmem_limit_bytes=24 << 20),
+    )(vec, link_rows)
     vmem = pl.BlockSpec(memory_space=pltpu.VMEM)
     return pl.pallas_call(
         fine_kernel,
-        in_specs=[vmem] * 6,
+        in_specs=[vmem] * 5,
         out_specs=vmem,
         out_shape=jax.ShapeDtypeStruct((ROWS, WIDE), jnp.bfloat16),
         scratch_shapes=[
@@ -313,13 +334,17 @@
             pltpu.VMEM((AT, NV, LANES), jnp.float32),
             pltpu.VMEM((8 * GROUP, LANES), jnp.float32),
             pltpu.VMEM((9, 8 * ROWS, LANES), jnp.float32),
+            pltpu.VMEM((4, 2, 512, LANES), jnp.bfloat16),
+            pltpu.VMEM((72, sites), jnp.float32),
+            pltpu.VMEM((144, sites), jnp.float32),
+            pltpu.VMEM((ROWS, LANES), jnp.float32),
             pltpu.SemaphoreType.DMA((6,)),
             pltpu.SemaphoreType.DMA((6,)),
         ],
         compiler_params=pltpu.CompilerParams(
             collective_id=2, has_side_effects=True, vmem_limit_bytes=32 << 20
         ),
-    )(faces, vec, link_f, site_f, tiled, table)
+    )(faces, vec, link_rows, site_rows, rhs)
 
 
 def complex_mul(first, second):
@@ -588,8 +613,11 @@
     return jnp.where(row % 2 == 0, pltpu.roll(value, count - 1, 0), pltpu.roll(value, 1, 0))
 
 
-def gmres_kernel(sizes, pick_ref, rows_ref, reduce_ref, op_ref, sol_ref, acc_ref, one_ref, two_ref):
-    size_z, size_y, size_x = sizes
+def gmres_kernel(
+    owner_ref, rows_ref, reduce_ref, op_ref, sol_ref, acc_ref, one_ref, two_ref, out_ref
+):
+    size_z, size_y, size_x = owner_ref.shape[:3]
+    me = lax.axis_index("gz") * size_x + lax.axis_index("gx")
     devices = size_z * size_y * size_x
     count = devices * ROWS
     row = lax.broadcasted_iota(jnp.int32, (count, LANES), 0)
@@ -651,12 +679,18 @@
             low, reduce_ref[...], preferred_element_type=jnp.float32
         )
 
+    def chosen_of(z, y, x):
+        chosen = jnp.int32(-1)
+        for a in range(AT):
+            chosen = jnp.where(owner_ref[z, y, x, a] == me, a, chosen)
+        return chosen
+
     for z in range(size_z):
         for y in range(size_y):
             for x in range(size_x):
                 at = (z * size_y + y) * size_x + x
                 place = (z * size_x + x) * size_y + y
-                chosen = pick_ref[at]
+                chosen = chosen_of(z, y, x)
 
                 @pl.when(chosen < 0)
                 def _():
@@ -718,15 +752,20 @@
             - weights[column][1] * (swapped[column] * sign)
         )
     one_ref[...] = answer
+    out_ref[...] = jnp.zeros(out_ref.shape, jnp.float32)
     for z in range(size_z):
         for y in range(size_y):
             for x in range(size_x):
                 at = (z * size_y + y) * size_x + x
-                chosen = pick_ref[at]
+                chosen = chosen_of(z, y, x)
                 shift = (ROWS - 2 * jnp.maximum(chosen, 0)) % ROWS
                 rows = pltpu.roll(one_ref[at * ROWS : (at + 1) * ROWS], shift, 0)
                 rows = jnp.where(chosen >= 0, rows, 0.0)
-                sol_ref[(z * size_x + x) * size_y + y] = rows[:2, :NV]
+                place = (z * size_x + x) * size_y + y
+                for part in range(2):
+                    out_ref[part, place : place + 1] = rows[part : part + 1]
+    for part in range(2):
+        sol_ref[part] = jnp.transpose(out_ref[part])[:NV, :devices]
 
 
 def reduce_table():
@@ -741,16 +780,13 @@
 
 
 def coarse_solve(rows, owner):
-    sizes = tuple(lax.axis_size(name) for name in ("gz", "gy", "gx"))
     devices, count = rows.shape[0], rows.shape[0] * ROWS
-    mine = owner.reshape(-1, AT) == lax.axis_index(("gz", "gx"))
-    chosen = jnp.max(jnp.where(mine, jnp.arange(AT, dtype=jnp.int32), -1), axis=1)
     vmem = pl.BlockSpec(memory_space=pltpu.VMEM)
     return pl.pallas_call(
-        lambda *refs: gmres_kernel(sizes, *refs),
+        gmres_kernel,
         out_shape=(
             jax.ShapeDtypeStruct((devices, 9, 2, NV * NV), jnp.bfloat16),
-            jax.ShapeDtypeStruct((devices, 2, NV), jnp.float32),
+            jax.ShapeDtypeStruct((2, NV, devices), jnp.float32),
         ),
         in_specs=[pl.BlockSpec(memory_space=pltpu.SMEM), vmem, vmem],
         out_specs=[vmem, vmem],
@@ -758,9 +794,10 @@
             pltpu.VMEM((count, CHUNKS * LANES), jnp.float32),
             pltpu.VMEM((count, LANES), jnp.float32),
             pltpu.VMEM((count, LANES), jnp.float32),
+            pltpu.VMEM((2, -(-devices // LANES) * LANES, LANES), jnp.float32),
         ],
-        compiler_params=pltpu.CompilerParams(vmem_limit_bytes=60 << 20),
-    )(chosen, rows, reduce_table())
+        compiler_params=pltpu.CompilerParams(vmem_limit_bytes=28 << 20),
+    )(owner, rows, reduce_table())
 
 
 def on_device(vectors, links, site_term, owner, coarse_rhs):
@@ -769,7 +806,7 @@
     )
     rows = gather_messages(message)
     operator, answer = coarse_solve(rows, owner)
-    return operator[None], answer[None]
+    return operator[None], jnp.transpose(answer, (2, 0, 1))[None]
 
 
 def solution(mesh):

time: 66.7 us -> 60.3 us (0.904)
  local copies, waits for them, and re-layouts: 8.1 us -> 1.57 us
  other arithmetic: 0.93 us -> 0 us
  Pallas kernels: 56.4 us -> 57.3 us
    unnamed x9 -> x10, local copies, waits for them, and re-layouts: 5.01 us -> 0.03 us
    transpose x1, local copies, waits for them, and re-layouts: 0.24 us -> 1.54 us  [fine_message(): vec = jnp.transpose(vectors, (0, 2, 3, 4, 1, 5)).reshape(AT, 24, NV, sites)]
    convert_element_type x4 -> x0, local copies, waits for them, and re-layouts: 1.29 us -> none  [the longest x2 1.03 us: fine_message(): link_f = links.astype(jnp.float32).reshape(AT, 72, sites)]
    concatenate x1 -> x0, local copies, waits for them, and re-layouts: 0.96 us -> none  [fine_message(): jnp.concatenate([rhs.reshape(ROWS, NV)] * GROUP + [jnp.zeros((ROWS, LANES...]
    reduce_max x1 -> x0, other arithmetic: 0.93 us -> none  [coarse_solve(): jnp.max(jnp.where(mine, jnp.arange(AT, dtype=jnp.int32), -1), axis=1)]
    pallas_call x2, Pallas kernels: 32.8 us -> 33.5 us  [the longest x1 18.2 us: fine_message(): pl.pallas_call(fine_kernel, in_specs=[vmem] * 5, out_specs=vmem, out_shap...]
where the time goes in v3:
time: 60.3 us; the launch traced here: 59.7 us
  Pallas kernels  57.3 us (95%)
  local copies, waits for them, and re-layouts  1.57 us (3%)
  between operations  0.74 us (1%)
    pallas_call x1, Pallas kernels, gather_messages(): pl.pallas_call(gather_kernel, out_shape=jax.ShapeDtypeStruct((devices, RO...  21.6 us
    pallas_call x1, Pallas kernels, fine_message(): pl.pallas_call(fine_kernel, in_specs=[vmem] * 5, out_specs=vmem, out_shap...  18.2 us
    pallas_call x1, Pallas kernels, coarse_solve(): pl.pallas_call(gmres_kernel, out_shape=(jax.ShapeDtypeStruct((devices, 9,...  15.2 us
    pallas_call x1, Pallas kernels, fine_message(): pl.pallas_call(faces_kernel, grid=(AT,), in_specs=[pl.BlockSpec((1, 24, N...  2.28 us
    transpose x1, local copies, waits for them, and re-layouts, fine_message(): vec = jnp.transpose(vectors, (0, 2, 3, 4, 1, 5)).reshape(AT, 24, NV, sites)  1.54 us

profile of v3, /device:TPU:0, one launch (start us, length us, event | category | flops | bytes accessed | tf_op | source)
XLA Modules:
  0.0 59.7 jit_solution(17197511137178717842)
XLA Ops:
  0.6 0.0 copy-start
  0.6 1.5 %copy.8 = bf16[4,2,4,3,24,256]{5,4,3,2,1,0:T(8,128)(2,1)S(1)} copy(bf16[4,2,4,3,24,256]{5,2,3,1,4,0:T(4,128)(2,1)} %bitcast.21) | data formatting | bytes 2359296 | tf_op jit(solution)/shard_map/transpose | solution.py:304
  2.2 0.0 copy-start.1
  2.2 0.0 copy-start.4
  2.2 0.0 copy-done
  2.2 2.3 %shard_map.77.face_ref = bf16[6,4,48,384]{3,2,1,0:T(8,128)(2,1)S(1)} custom-call(bf16[4,24,24,256]{3,2,1,0:T(8,128)(2,1)S(1)} %bitcast.15, bf16[4,4,3,3,2,256]{5,4,3,2,1,0:T(2,128)(2,1)S(1)} %bitcast.17), custom_call_target="tpu_custom_call" | custom-call | tf_op jit(solution)/shard_map/pallas_call | solution.py:308
  4.5 0.0 copy-done.1
  4.5 0.0 copy-done.4
  4.5 18.2 %shard_map.78.msg_ref = bf16[8,5888]{1,0:T(8,128)(2,1)S(1)} custom-call(bf16[6,4,48,384]{3,2,1,0:T(8,128)(2,1)S(1)} %shard_map.77.face_ref, bf16[4,24,24,256]{3,2,1,0:T(8,128)(2,1)S(1)} %bitcast.16, bf16[4,4,3,3,2,256]{5,4,3,2,1,0:T(2,128)(2,1)S(1)} %bitcast.18, bf16[4,2,6,6,2,256]{5,4,3,2,1,0:T(2,128)(2,1)S(1)} %bitcast.19, bf16[4,2,24]{2,1,0:T(2,128)(2,1)S(1)} %bitcast.20), custom_call_target="tpu_custom_call" | custom-call | tf_op jit(solution)/shard_map/pallas_call | solution.py:324
  22.8 0.0 copy-start.2
  22.8 0.0 copy-start.3
  22.8 21.6 %shard_map.79.rows_ref = bf16[32,8,5888]{2,1,0:T(8,128)(2,1)S(1)} custom-call(bf16[8,5888]{1,0:T(8,128)(2,1)S(1)} %shard_map.78.msg_ref), custom_call_target="tpu_custom_call" | custom-call | tf_op jit(solution)/shard_map/pallas_call | solution.py:587
  44.4 0.0 copy-done.2
  44.4 0.0 copy-done.3
  44.4 15.2 %shard_map.80 = (bf16[32,9,2,576]{3,2,1,0:T(2,128)(2,1)}, f32[2,24,32]{2,1,0:T(8,128)}) custom-call(s32[4,2,4,4]{3,2,1,0:T(4,128)S(1)} %copy-done.3, bf16[32,8,5888]{2,1,0:T(8,128)(2,1)S(1)} %shard_map.79.rows_ref, bf16[640,128]{1,0:T(8,128)(2,1)S(1)} %copy-done.2), custom_call_target="tpu_custom_call" | custom-call | tf_op jit(solution)/shard_map/pallas_call | solution.py:785
Async XLA Ops:
  0.6 1.6 %copy-start = (bf16[1,1,1,4,4,2,3,3,256]{8,5,7,6,4,3,2,1,0:T(2,128)(2,1)S(1)}, bf16[1,1,1,4,4,2,3,3,256]{8,5,7,6,4,3,2,1,0:T(2,128)(2,1)}, u32[]{:S(2)}) copy-start(bf16[1,1,1,4,4,2,3,3,256]{8,5,7,6,4,3,2,1,0:T(2,128)(2,1)} %param.7) | copy-start | bytes 442372
  2.2 2.3 %copy-start.1 = (bf16[1,1,1,4,2,2,6,6,256]{8,5,7,6,4,3,2,1,0:T(2,128)(2,1)S(1)}, bf16[1,1,1,4,2,2,6,6,256]{8,5,7,6,4,3,2,1,0:T(2,128)(2,1)}, u32[]{:S(2)}) copy-start(bf16[1,1,1,4,2,2,6,6,256]{8,5,7,6,4,3,2,1,0:T(2,128)(2,1)} %param.8) | copy-start | bytes 884740
  2.2 2.3 %copy-start.4 = (bf16[1,1,1,4,2,24]{5,4,3,2,1,0:T(2,128)(2,1)S(1)}, bf16[1,1,1,4,2,24]{5,4,3,2,1,0:T(2,128)(2,1)}, u32[]{:S(2)}) copy-start(bf16[1,1,1,4,2,24]{5,4,3,2,1,0:T(2,128)(2,1)} %param.10) | copy-start | bytes 1156
  22.8 21.7 %copy-start.2 = (bf16[640,128]{1,0:T(8,128)(2,1)S(1)}, bf16[640,128]{1,0:T(8,128)(2,1)}, u32[]{:S(2)}) copy-start(bf16[640,128]{1,0:T(8,128)(2,1)} %constant.2.clone.reduce_ref) | copy-start | bytes 491524
  22.8 21.6 %copy-start.3 = (s32[4,2,4,4]{3,2,1,0:T(4,128)S(1)}, s32[4,2,4,4]{3,2,1,0:T(4,128)}, u32[]{:S(2)}) copy-start(s32[4,2,4,4]{3,2,1,0:T(4,128)} %owner_ref.1) | copy-start | bytes 1540
